TPU v7x, 128 devices: a whole 4x4x4 slice. The times are simulated.
128 devices in a mesh: orb: 8 (over z, core), pair: 16 (over y, x).
Axes of the slice: x: 4, y: 4, z: 4, core: 2. Of those that a mesh axis runs over, the one named last changes fastest.
Arguments:
- blocks: bfloat16 [512, 1024, 320], P(('orb', 'pair')), may hold values from -1.1953125 to 1.1953125
- aux_domain: int32 [512, 1024], replicated, may hold values from 0 to 2047, as said below
- pao_domain: int32 [512, 320], replicated, may hold values from -1 to 639, as said below
- pao_gap: float32 [512, 320], replicated, may hold values from 1 to 4
- amplitudes: bfloat16 [1024, 320, 320], P(('orb', 'pair')), may hold values from -3 to 3
- pair_partner: int32 [1024], replicated, may hold values from 0 to 511, as said below
- coupling_list: int32 [1024, 4], P(('orb', 'pair')), may hold values from 0 to 1023, as said below
- coupling_coef: float32 [1024, 4], P(('orb', 'pair')), may hold values from -0.6 to 0.6
Outputs:
- new_amplitudes: bfloat16 [1024, 320, 320], P(('orb', 'pair'))
- pair_energy: float32 [1024], P(('orb', 'pair'))
- densities: float32 [512, 320, 320], P(('orb', 'pair'))
Inputs may be any that keep to these rules, and one draw needn't show every extreme that they name: `aux_domain`: each row holds 1024 distinct auxiliary function ids. `pao_domain`: each row holds distinct PAO ids in its leading slots and -1 in the rest; at least 160 ids a row. With d = p // 8, pair_partner[p] lies in [(d - 1) * 4, (d + 2) * 4). `coupling_list`: row p lists pair ids q with 0 < |q - p| <= 8.
All inputs are finite; a program needn't handle non-finite values.
Results may differ from a plain program's by a relative error of at most 0.003.
Values may be sent and summed in bfloat16 or wider, within the bound.
A program may use at most 128 MiB of HBM per device.

v0:
```python
import jax
import jax.numpy as jnp
from jax import lax
from jax.sharding import PartitionSpec as P

OCC_DEV = 4
PAIR_DEV = 8


def with_halo(array, sides, width):
    for axis, dim in sides:
        peers, length = (lax.axis_size(axis), array.shape[dim])
        up = [(i, (i + 1) % peers) for i in range(peers - 1)]
        down = [(j, i) for i, j in up]
        last = lax.slice_in_dim(array, length - width, length, axis=dim)
        initial = lax.slice_in_dim(array, 0, width, axis=dim)
        before = lax.ppermute(last, axis, up)
        after = lax.ppermute(initial, axis, down)
        array = jnp.concatenate([before, array, after], axis=dim)
    return array


def passed_along(block, axis, distance):
    devices = range(lax.axis_size(axis))
    route = [(i - distance, i) for i in devices if i - distance in devices]
    return lax.ppermute(block, axis, route)


def first_orbital(pair_id):
    return pair_id // PAIR_DEV * OCC_DEV + pair_id % OCC_DEV


def selector(wanted, present):
    equal = (wanted[:, None] == present[None, :]) & (wanted[:, None] >= 0)
    return equal.astype(jnp.bfloat16)


def pair_terms(
    left_block,
    right_block,
    aux_left,
    aux_right,
    pao_left,
    pao_right,
    gap_left,
    gap_right,
    amp,
    near_amps,
    near_left,
    near_right,
    coefs,
):
    aligned = jnp.dot(
        selector(aux_left, aux_right), right_block, preferred_element_type=jnp.float32
    ).astype(jnp.bfloat16)
    mask_left = (pao_left >= 0).astype(jnp.float32)
    mask_right = (pao_right >= 0).astype(jnp.float32)
    both = mask_left[:, None] * mask_right[None, :]
    exchange = (
        lax.dot_general(
            left_block, aligned, (((0,), (0,)), ((), ())), preferred_element_type=jnp.float32
        )
        * both
    )
    masked = (amp.astype(jnp.float32) * both).astype(jnp.bfloat16)

    def project(near_amp, pao_near_left, pao_near_right, coef):
        rows = jnp.dot(
            selector(pao_left, pao_near_left), near_amp, preferred_element_type=jnp.float32
        ).astype(jnp.bfloat16)
        picked = lax.dot_general(
            rows,
            selector(pao_right, pao_near_right),
            (((1,), (1,)), ((), ())),
            preferred_element_type=jnp.float32,
        )
        return coef * picked

    coupling = jnp.sum(jax.vmap(project)(near_amps, near_left, near_right, coefs), axis=0)
    denom = gap_left[:, None] + gap_right[None, :]
    masked_f = masked.astype(jnp.float32)
    residual = exchange + denom * masked_f - coupling
    new_amp = (masked_f - 0.5 * residual / denom).astype(jnp.bfloat16)
    energy = jnp.sum(exchange * masked_f) / masked.shape[0]
    return (new_amp, energy, masked)


def left_density(masked):
    return (
        lax.dot_general(
            masked, masked, (((1,), (1,)), ((), ())), preferred_element_type=jnp.float32
        )
        / masked.shape[0]
    )


def right_density(masked):
    return (
        lax.dot_general(
            masked, masked, (((0,), (0,)), ((), ())), preferred_element_type=jnp.float32
        )
        / masked.shape[0]
    )


def local(
    blocks, aux_domain, pao_domain, pao_gap, amplitudes, pair_partner, coupling_list, coupling_coef
):
    here = lax.axis_index(("orb", "pair"))
    occ_local = blocks.shape[0]
    pairs_local = amplitudes.shape[0]
    width = amplitudes.shape[1]
    wide_blocks = with_halo(blocks, ((("orb", "pair"), 0),), occ_local)
    wide_amps = with_halo(amplitudes, ((("orb", "pair"), 0),), pairs_local)
    orbital_base = (here - 1) * occ_local
    pair_base = (here - 1) * pairs_local
    local_ids = here * pairs_local + jnp.arange(pairs_local, dtype=jnp.int32)

    def one_pair(items):
        pair_id, amp, neighbours, coefs = items
        left = first_orbital(pair_id)
        right = pair_partner[pair_id]
        left_block = lax.dynamic_index_in_dim(wide_blocks, left - orbital_base, 0, keepdims=False)
        right_block = lax.dynamic_index_in_dim(wide_blocks, right - orbital_base, 0, keepdims=False)
        near_amps = jnp.take(wide_amps, neighbours - pair_base, axis=0)
        near_left = pao_domain[first_orbital(neighbours)]
        near_right = pao_domain[pair_partner[neighbours]]
        new_amp, energy, masked = pair_terms(
            left_block,
            right_block,
            aux_domain[left],
            aux_domain[right],
            pao_domain[left],
            pao_domain[right],
            pao_gap[left],
            pao_gap[right],
            amp,
            near_amps,
            near_left,
            near_right,
            coefs,
        )
        return (new_amp, energy, masked, left_density(masked))

    new_amps, energies, masked_all, left_terms = lax.map(
        one_pair, (local_ids, amplitudes, coupling_list, coupling_coef)
    )
    densities = jnp.sum(
        left_terms.reshape(pairs_local // occ_local, occ_local, width, width), axis=0
    )
    right_terms = lax.map(right_density, masked_all)
    spots = pair_partner[local_ids] - orbital_base
    table = (spots[:, None] == jnp.arange(3 * occ_local)[None, :]).astype(jnp.float32)
    spread = jnp.einsum("pe,pab->eab", table, right_terms, precision=lax.Precision.HIGHEST)
    from_before = passed_along(
        spread[2 * occ_local :].astype(jnp.bfloat16), ("orb", "pair"), 1
    ).astype(jnp.float32)
    from_after = passed_along(spread[:occ_local].astype(jnp.bfloat16), ("orb", "pair"), -1).astype(
        jnp.float32
    )
    densities = densities + spread[occ_local : 2 * occ_local] + from_before + from_after
    return (new_amps, energies, densities)


def solution(mesh):
    return jax.shard_map(
        local,
        mesh=mesh,
        in_specs=(
            P(("orb", "pair"), None, None),
            P(),
            P(),
            P(),
            P(("orb", "pair"), None, None),
            P(),
            P(("orb", "pair"), None),
            P(("orb", "pair"), None),
        ),
        out_specs=(
            P(("orb", "pair"), None, None),
            P(("orb", "pair")),
            P(("orb", "pair"), None, None),
        ),
        check_vma=False,
    )
```

profile of v0, /device:TPU:96, one launch (start us, length us, event | category | flops | bytes accessed | tf_op | source)
XLA Modules:
  0.0 494.0 jit_solution(16035925697982146590)
XLA Ops:
  0.7 3.5 collective-permute-start
  4.2 6.4 %collective-permute-start.1 = (bf16[4,1024,320]{1,2,0:T(8,128)(2,1)}, bf16[4,1024,320]{1,2,0:T(8,128)(2,1)}, u32[]{:S(2)}, u32[]{:S(2)}) collective-permute-start(bf16[4,1024,320]{1,2,0:T(8,128)(2,1)} %param.12), channel_id=1, source_target_pairs={{1,0},{2,1},{3,2},{4,3},{5,4},{6,5},{7,6},{8,7},{9,8},{10,9},{11,1... | collective-permute-start | bytes 7864328 | tf_op jit(solution)/shard_map/ppermute | solution.py:18
  10.6 1.9 collective-permute-start.2
  12.5 7.9 %collective-permute-start.3 = (bf16[8,320,320]{2,1,0:T(8,128)(2,1)}, bf16[8,320,320]{2,1,0:T(8,128)(2,1)}, u32[]{:S(2)}, u32[]{:S(2)}) collective-permute-start(bf16[8,320,320]{2,1,0:T(8,128)(2,1)} %param.16), channel_id=1, source_target_pairs={{1,0},{2,1},{3,2},{4,3},{5,4},{6,5},{7,6},{8,7},{9,8},{10,9},{11,1... | collective-permute-start | bytes 4915208 | tf_op jit(solution)/shard_map/ppermute | solution.py:18
  20.5 2.3 copy.28
  22.7 2.3 copy.30
  25.8 82.1 %collective-permute-done.2 = bf16[8,320,320]{2,1,0:T(8,128)(2,1)} collective-permute-done((bf16[8,320,320]{2,1,0:T(8,128)(2,1)}, bf16[8,320,320]{2,1,0:T(8,128)(2,1)}, u32[]{:S(2)}, u32[]{:S(2)}) %collective-permute-start.2) | collective-permute-done | bytes 1638432 | tf_op jit(solution)/shard_map/ppermute | solution.py:17
  109.0 5.7 %pad_maximum_fusion.1 = bf16[24,320,320]{2,1,0:T(8,128)(2,1)} fusion(bf16[8,320,320]{2,1,0:T(8,128)(2,1)} %collective-permute-done.3, bf16[8,320,320]{2,1,0:T(8,128)(2,1)S(1)} %copy-done.1, bf16[8,320,320]{2,1,0:T(8,128)(2,1)} %collective-permute-done.2), kind=kLoop, calls=%fused_computation.104 | loop fusion | flops 4915200 | bytes 9830400 | tf_op jit(solution)/shard_map/concatenate | solution.py:19
  114.7 6.3 %pad_maximum_fusion = bf16[12,1024,320]{1,2,0:T(8,128)(2,1)} fusion(bf16[4,1024,320]{1,2,0:T(8,128)(2,1)} %collective-permute-done.1, bf16[4,1024,320]{1,2,0:T(8,128)(2,1)S(1)} %copy-done.2, bf16[4,1024,320]{1,2,0:T(8,128)(2,1)} %collective-permute-done), kind=kLoop, calls=%fused_computation.103 | loop fusion | flops 7864320 | bytes 15728640 | tf_op jit(solution)/shard_map/concatenate | solution.py:19
  121.0 11.6 %copy.29 = bf16[12,1024,320]{2,1,0:T(8,128)(2,1)} copy(bf16[12,1024,320]{1,2,0:T(8,128)(2,1)} %pad_maximum_fusion) | data formatting | bytes 15728640 | tf_op jit(solution)/shard_map/while | solution.py:145
  132.6 209.6 %while.29 = (s32[]{:T(128)}, bf16[8,320,320]{2,1,0:T(8,128)(2,1)}, f32[8]{0:T(128)S(1)}, bf16[8,320,320]{2,1,0:T(8,128)(2,1)}, f32[8,320,320]{2,1,0:T(8,128)}, /...) while((s32[]{:T(128)}, bf16[8,320,320]{2,1,0:T(8,128)(2,1)}, ...), condition=%wide.region_3.4_spmd, body=%wide.region_0.3_spmd.sunk | while | flops 1479203584 | bytes 7550051 | solution.py:145
  143.1 3.4 gather_fusion.2
  146.5 1.7 gather_fusion.3
  152.0 3.8 fusion.125
  169.2 3.4 gather_fusion.2
  172.7 1.7 gather_fusion.3
  178.2 3.8 fusion.125
  195.4 3.4 gather_fusion.2
  204.3 3.8 fusion.125
  221.5 3.4 gather_fusion.2
  230.6 3.8 fusion.125
  247.8 3.4 gather_fusion.2
  251.3 1.7 gather_fusion.3
  256.9 3.8 fusion.125
  274.1 3.4 gather_fusion.2
  277.5 1.7 gather_fusion.3
  283.0 3.8 fusion.125
  300.3 3.4 gather_fusion.2
  303.7 1.7 gather_fusion.3
  309.3 3.8 fusion.125
  326.5 3.4 gather_fusion.2
  335.4 3.8 fusion.125
  342.7 105.9 %while.30 = (s32[]{:T(128)}, f32[8,320,320]{2,0,1:T(8,128)}, bf16[8,320,320]{2,1,0:T(8,128)(2,1)}, s32[]{:T(128)}, s32[]{:T(128)}) while((s32[]{:T(128)}, f32[8,320,320]{2,0,1:T(8,128)}, bf16[8,320,320]{2,1,0:T(8,128)(2,1)}, s32[]{:T(128)}, s32[]{:T(128)}) %tuple.85), condition=%wide.region_6.7_spmd, body=%wide.region_5.6_spmd.sunk | while | flops 65638400 | bytes 2294337 | solution.py:151
  344.6 11.3 %dynamic_update_slice.44 = f32[8,320,320]{2,0,1:T(8,128)} dynamic-update-slice(f32[8,320,320]{2,0,1:T(8,128)} %get-tuple-element.659, f32[1,320,320]{2,0,1:T(1,128)S(1)} %copy.41, s32[]{:T(128)} %get-tuple-element.658, s32[]{:T(128)} %constant.205.clone.1..sunk.1, s32[]{:T(128)} %constant.205.clone.1..sunk.1) | dynamic-update-slice | bytes 819204 | tf_op jit(solution)/shard_map/while/body/jit(dynamic_update_index_in_dim)/dynamic_update_slice | solution.py:145
  357.8 11.3 %dynamic_update_slice.44 = f32[8,320,320]{2,0,1:T(8,128)} dynamic-update-slice(f32[8,320,320]{2,0,1:T(8,128)} %get-tuple-element.659, f32[1,320,320]{2,0,1:T(1,128)S(1)} %copy.41, s32[]{:T(128)} %get-tuple-element.658, s32[]{:T(128)} %constant.205.clone.1..sunk.1, s32[]{:T(128)} %constant.205.clone.1..sunk.1) | dynamic-update-slice | bytes 819204 | tf_op jit(solution)/shard_map/while/body/jit(dynamic_update_index_in_dim)/dynamic_update_slice | solution.py:145
  371.1 11.3 %dynamic_update_slice.44 = f32[8,320,320]{2,0,1:T(8,128)} dynamic-update-slice(f32[8,320,320]{2,0,1:T(8,128)} %get-tuple-element.659, f32[1,320,320]{2,0,1:T(1,128)S(1)} %copy.41, s32[]{:T(128)} %get-tuple-element.658, s32[]{:T(128)} %constant.205.clone.1..sunk.1, s32[]{:T(128)} %constant.205.clone.1..sunk.1) | dynamic-update-slice | bytes 819204 | tf_op jit(solution)/shard_map/while/body/jit(dynamic_update_index_in_dim)/dynamic_update_slice | solution.py:145
  384.3 11.3 %dynamic_update_slice.44 = f32[8,320,320]{2,0,1:T(8,128)} dynamic-update-slice(f32[8,320,320]{2,0,1:T(8,128)} %get-tuple-element.659, f32[1,320,320]{2,0,1:T(1,128)S(1)} %copy.41, s32[]{:T(128)} %get-tuple-element.658, s32[]{:T(128)} %constant.205.clone.1..sunk.1, s32[]{:T(128)} %constant.205.clone.1..sunk.1) | dynamic-update-slice | bytes 819204 | tf_op jit(solution)/shard_map/while/body/jit(dynamic_update_index_in_dim)/dynamic_update_slice | solution.py:145
  397.6 11.3 %dynamic_update_slice.44 = f32[8,320,320]{2,0,1:T(8,128)} dynamic-update-slice(f32[8,320,320]{2,0,1:T(8,128)} %get-tuple-element.659, f32[1,320,320]{2,0,1:T(1,128)S(1)} %copy.41, s32[]{:T(128)} %get-tuple-element.658, s32[]{:T(128)} %constant.205.clone.1..sunk.1, s32[]{:T(128)} %constant.205.clone.1..sunk.1) | dynamic-update-slice | bytes 819204 | tf_op jit(solution)/shard_map/while/body/jit(dynamic_update_index_in_dim)/dynamic_update_slice | solution.py:145
  410.8 11.3 %dynamic_update_slice.44 = f32[8,320,320]{2,0,1:T(8,128)} dynamic-update-slice(f32[8,320,320]{2,0,1:T(8,128)} %get-tuple-element.659, f32[1,320,320]{2,0,1:T(1,128)S(1)} %copy.41, s32[]{:T(128)} %get-tuple-element.658, s32[]{:T(128)} %constant.205.clone.1..sunk.1, s32[]{:T(128)} %constant.205.clone.1..sunk.1) | dynamic-update-slice | bytes 819204 | tf_op jit(solution)/shard_map/while/body/jit(dynamic_update_index_in_dim)/dynamic_update_slice | solution.py:145
  424.0 11.3 %dynamic_update_slice.44 = f32[8,320,320]{2,0,1:T(8,128)} dynamic-update-slice(f32[8,320,320]{2,0,1:T(8,128)} %get-tuple-element.659, f32[1,320,320]{2,0,1:T(1,128)S(1)} %copy.41, s32[]{:T(128)} %get-tuple-element.658, s32[]{:T(128)} %constant.205.clone.1..sunk.1, s32[]{:T(128)} %constant.205.clone.1..sunk.1) | dynamic-update-slice | bytes 819204 | tf_op jit(solution)/shard_map/while/body/jit(dynamic_update_index_in_dim)/dynamic_update_slice | solution.py:145
  437.3 11.3 %dynamic_update_slice.44 = f32[8,320,320]{2,0,1:T(8,128)} dynamic-update-slice(f32[8,320,320]{2,0,1:T(8,128)} %get-tuple-element.659, f32[1,320,320]{2,0,1:T(1,128)S(1)} %copy.41, s32[]{:T(128)} %get-tuple-element.658, s32[]{:T(128)} %constant.205.clone.1..sunk.1, s32[]{:T(128)} %constant.205.clone.1..sunk.1) | dynamic-update-slice | bytes 819204 | tf_op jit(solution)/shard_map/while/body/jit(dynamic_update_index_in_dim)/dynamic_update_slice | solution.py:145
  448.6 7.1 %fusion.94 = (bf16[12,320,320]{2,0,1:T(8,128)(2,1)S(1)}, f32[12,320,320]{2,0,1:T(8,128)}) fusion(f32[8,320,320]{2,0,1:T(8,128)} %get-tuple-element.285, s32[8]{0:T(128)S(1)} %broadcast_subtract_fusion), kind=kOutput, calls=%fused_computation.119 | convolution fusion | flops 119193696 | bytes 10649632 | tf_op jit(solution)/shard_map/pe,pab->eab/dot_general | solution.py:154
  455.7 1.9 fusion.93
  457.6 1.9 collective-permute-start.4
  459.5 8.4 %collective-permute-start.5 = (bf16[4,320,320]{2,0,1:T(4,128)(2,1)}, bf16[4,320,320]{2,0,1:T(4,128)(2,1)}, u32[]{:S(2)}, u32[]{:S(2)}) collective-permute-start(bf16[4,320,320]{2,0,1:T(4,128)(2,1)} %get-tuple-element.407), channel_id=1, source_target_pairs={{1,0},{2,1},{3,2},{4,3},{5,4},{6,5},{7,6},{8,7},{9,8},{10,9},{11,1... | collective-permute-start | bytes 2457608 | tf_op jit(solution)/shard_map/ppermute | solution.py:26
  467.9 2.6 reduce_sum.35
  470.5 16.4 %collective-permute-done.4 = bf16[4,320,320]{2,0,1:T(4,128)(2,1)S(1)} collective-permute-done((bf16[4,320,320]{2,0,1:T(4,128)(2,1)}, bf16[4,320,320]{2,0,1:T(4,128)(2,1)S(1)}, u32[]{:S(2)}, u32[]{:S(2)}) %collective-permute-start.4) | collective-permute-done | bytes 819232 | tf_op jit(solution)/shard_map/ppermute | solution.py:26
  488.4 4.2 fusion.82
  (208 shorter events, 104.3 us)
Async XLA Ops:
  0.6 108.3 %copy-start.1 = (bf16[8,320,320]{2,1,0:T(8,128)(2,1)S(1)}, bf16[8,320,320]{2,1,0:T(8,128)(2,1)}, u32[]{:S(2)}) copy-start(bf16[8,320,320]{2,1,0:T(8,128)(2,1)} %param.16) | copy-start | bytes 4915204
  0.6 24.4 %copy-start.3 = (f32[8,4]{0,1:T(4,128)S(1)}, f32[8,4]{0,1:T(4,128)}, u32[]{:S(2)}) copy-start(f32[8,4]{0,1:T(4,128)} %param.19) | copy-start | bytes 388
  0.7 24.4 %copy-start.4 = (s32[8,4]{0,1:T(4,128)S(1)}, s32[8,4]{0,1:T(4,128)}, u32[]{:S(2)}) copy-start(s32[8,4]{0,1:T(4,128)} %param.18) | copy-start | bytes 388
  0.7 24.5 %copy-start = (s32[1024]{0:T(1024)S(1)}, s32[1024]{0:T(1024)}, u32[]{:S(2)}) copy-start(s32[1024]{0:T(1024)} %param.17) | copy-start | bytes 12292
  0.7 114.0 %collective-permute-start = (bf16[4,1024,320]{1,2,0:T(8,128)(2,1)}, bf16[4,1024,320]{1,2,0:T(8,128)(2,1)}, u32[]{:S(2)}, u32[]{:S(2)}) collective-permute-start(bf16[4,1024,320]{1,2,0:T(8,128)(2,1)} %param.12), channel_id=1, source_target_pairs={{0,1},{1,2},{2,3},{3,4},{4,5},{5,6},{6,7},{7,8},{8,9},{9,10},{10,1... | collective-permute-start | bytes 7864328 | tf_op jit(solution)/shard_map/ppermute | solution.py:17
  4.2 110.5 %collective-permute-start.1 = (bf16[4,1024,320]{1,2,0:T(8,128)(2,1)}, bf16[4,1024,320]{1,2,0:T(8,128)(2,1)}, u32[]{:S(2)}, u32[]{:S(2)}) collective-permute-start(bf16[4,1024,320]{1,2,0:T(8,128)(2,1)} %param.12), channel_id=1, source_target_pairs={{1,0},{2,1},{3,2},{4,3},{5,4},{6,5},{7,6},{8,7},{9,8},{10,9},{11,1... | collective-permute-start | bytes 7864328 | tf_op jit(solution)/shard_map/ppermute | solution.py:18
  10.6 97.3 %collective-permute-start.2 = (bf16[8,320,320]{2,1,0:T(8,128)(2,1)}, bf16[8,320,320]{2,1,0:T(8,128)(2,1)}, u32[]{:S(2)}, u32[]{:S(2)}) collective-permute-start(bf16[8,320,320]{2,1,0:T(8,128)(2,1)} %param.16), channel_id=1, source_target_pairs={{0,1},{1,2},{2,3},{3,4},{4,5},{5,6},{6,7},{7,8},{8,9},{9,10},{10,1... | collective-permute-start | bytes 4915208 | tf_op jit(solution)/shard_map/ppermute | solution.py:17
  12.5 96.4 %collective-permute-start.3 = (bf16[8,320,320]{2,1,0:T(8,128)(2,1)}, bf16[8,320,320]{2,1,0:T(8,128)(2,1)}, u32[]{:S(2)}, u32[]{:S(2)}) collective-permute-start(bf16[8,320,320]{2,1,0:T(8,128)(2,1)} %param.16), channel_id=1, source_target_pairs={{1,0},{2,1},{3,2},{4,3},{5,4},{6,5},{7,6},{8,7},{9,8},{10,9},{11,1... | collective-permute-start | bytes 4915208 | tf_op jit(solution)/shard_map/ppermute | solution.py:18
  25.8 88.9 %copy-start.2 = (bf16[4,1024,320]{1,2,0:T(8,128)(2,1)S(1)}, bf16[4,1024,320]{1,2,0:T(8,128)(2,1)}, u32[]{:S(2)}) copy-start(bf16[4,1024,320]{1,2,0:T(8,128)(2,1)} %param.12) | copy-start | bytes 7864324
  342.2 0.5 copy-start.5
  457.6 29.3 %collective-permute-start.4 = (bf16[4,320,320]{2,0,1:T(4,128)(2,1)}, bf16[4,320,320]{2,0,1:T(4,128)(2,1)S(1)}, u32[]{:S(2)}, u32[]{:S(2)}) collective-permute-start(bf16[4,320,320]{2,0,1:T(4,128)(2,1)} %get-tuple-element.406), channel_id=1, source_target_pairs={{0,1},{1,2},{2,3},{3,4},{4,5},{5,6},{6,7},{7,8},{8,9},{9,10},{10,1... | collective-permute-start | bytes 2457608 | tf_op jit(solution)/shard_map/ppermute | solution.py:26
  459.5 28.9 %collective-permute-start.5 = (bf16[4,320,320]{2,0,1:T(4,128)(2,1)}, bf16[4,320,320]{2,0,1:T(4,128)(2,1)}, u32[]{:S(2)}, u32[]{:S(2)}) collective-permute-start(bf16[4,320,320]{2,0,1:T(4,128)(2,1)} %get-tuple-element.407), channel_id=1, source_target_pairs={{1,0},{2,1},{3,2},{4,3},{5,4},{6,5},{7,6},{8,7},{9,8},{10,9},{11,1... | collective-permute-start | bytes 2457608 | tf_op jit(solution)/shard_map/ppermute | solution.py:26
where the time goes:
time: 502 us; the launch traced here: 494 us
  local copies, waits for them, and re-layouts  199 us (40%)
  waiting for transfers between devices  101 us (20%)
  matrix products  70.6 us (14%)
  loops' own time  59.4 us (12%)
  other arithmetic  33 us (7%)
  starting transfers between devices  30 us (6%)
    dynamic_update_slice x24, local copies, waits for them, and re-layouts, local(): lax.map(one_pair, (local_ids, amplitudes, coupling_list, coupling_coef))  95.5 us
    ppermute x2, waiting for transfers between devices, with_halo(): before = lax.ppermute(last, axis, up)  82.1 us
    another operation x1, loops' own time, local(): lax.map(one_pair, (local_ids, amplitudes, coupling_list, coupling_coef))  59.2 us
    dot_general x8, matrix products, pair_terms(): lax.dot_general(left_block, aligned, (((0,), (0,)), ((), ())), preferred_...  30.6 us
    gather x8, local copies, waits for them, and re-layouts, one_pair(): near_amps = jnp.take(wide_amps, neighbours - pair_base, axis=0)  27.5 us
    gather x16, local copies, waits for them, and re-layouts, one_pair(): near_right = pao_domain[pair_partner[neighbours]]  18.6 us
    ppermute x2, waiting for transfers between devices, passed_along(): return lax.ppermute(block, axis, route)  17.9 us
    while x5, local copies, waits for them, and re-layouts, local(): lax.map(one_pair, (local_ids, amplitudes, coupling_list, coupling_coef))  16.3 us
  transfers between devices with their start and end apart: 6, of which 4 were waited for; matrix products, arithmetic and copies ran while one was open for 3% of the time, Pallas kernels for 0%

commit v1 on v0

v1 whole, which is shorter than its diff:
```python
import functools

import jax
import jax.numpy as jnp
from jax import lax
from jax.experimental import pallas as pl
from jax.experimental.pallas import tpu as pltpu
from jax.sharding import PartitionSpec as P


OCC_DEV = 4
PAIR_DEV = 8
NCPL = 4
AXES = ("orb", "pair")
F32 = jnp.float32
BF16 = jnp.bfloat16
MAIN = 256
CUTS = (0, 1, 3, 4)
ORDER_START, ORDER_COUNT, ORDER_SIZE = 16, 24, 32
CONTRACT_LAST = (((1,), (1,)), ((), ()))


def column(row, rows):
    wide = jnp.broadcast_to(row, (128, row.shape[1]))
    return wide.T[:rows]


def wanted(row):
    return jnp.where(row < 0, -2, row)


def lanes(col, row):
    pieces = [
        jnp.where(col == row[:, at : at + 128], F32(1), F32(0)).astype(BF16)
        for at in range(0, row.shape[1], 128)
    ]
    return pieces[0] if len(pieces) == 1 else jnp.concatenate(pieces, axis=1)


def mask_kernel(here, partner, tab_ref, low_ref, high_ref, out_ref, *, base_of):
    k = pl.program_id(0)
    rows = low_ref.shape[1]
    first = here[0] * OCC_DEV + k - base_of(here[0])
    left = column(tab_ref[pl.ds(first, 1), :], rows) >= 0

    def masked(amp, p, start, size):
        at = partner[here[0] * PAIR_DEV + p] - base_of(here[0])
        right = tab_ref[pl.ds(at, 1), :][:, start : start + size] >= 0
        keep = left[:, :1] & right
        return jnp.where(keep, amp[0, :, start : start + size].astype(F32), F32(0))

    rests = []
    for n, ref in enumerate((low_ref, high_ref)):
        p = k + n * OCC_DEV
        out_ref[0, :, n * MAIN : (n + 1) * MAIN] = masked(ref, p, 0, MAIN).astype(BF16)
        rests.append(masked(ref, p, MAIN, rows - MAIN))
    out_ref[0, :, 2 * MAIN :] = jnp.concatenate(rests, axis=1).astype(BF16)


def stage_of(spot):
    slot = lax.rem(spot, OCC_DEV)
    away = (spot // OCC_DEV) != 1
    return jnp.where(away & (slot >= CUTS[1]), jnp.where(slot >= CUTS[2], 2, 1), 0)


def align_kernel(here, partner, aux_ref, left_ref, out_ref, order_ref, col_ref, *, base_of):
    p = pl.program_id(0)

    @pl.when(p == 0)
    def _():
        total = jnp.int32(0)
        for stage in range(len(CUTS) - 1):
            start = total
            for q in range(PAIR_DEV):
                spot = partner[here[0] * PAIR_DEV + q] - (here[0] - 1) * OCC_DEV
                hit = stage_of(spot) == stage
                order_ref[jnp.where(hit, total, PAIR_DEV)] = q
                total = total + hit.astype(jnp.int32)
            order_ref[ORDER_COUNT + stage] = jnp.maximum(total - start, 1)
            order_ref[ORDER_START + stage] = start

    k = lax.rem(p, OCC_DEV)
    naux = left_ref.shape[2]
    base = base_of(here[0])
    first = here[0] * OCC_DEV + k - base
    col_ref[...] = column(aux_ref[pl.ds(first, 1), :], naux)
    second = partner[here[0] * PAIR_DEV + p] - base
    left = left_ref[0]
    present = aux_ref[pl.ds(second, 1), :]
    for at in range(0, naux, MAIN):
        pick = lanes(col_ref[...], present[:, at : at + MAIN])
        out_ref[0, :, at : at + MAIN] = jnp.dot(left, pick, preferred_element_type=F32).astype(BF16)


def coupling_kernel(
    here,
    partner,
    near,
    coef,
    tab_ref,
    prev_hbm,
    own_hbm,
    next_hbm,
    out_ref,
    dens_ref,
    amps,
    rows_ref,
    cols_ref,
    acc,
    sems,
    *,
    base_of,
):
    p = pl.program_id(0)
    me = here[0]
    base = base_of(me)
    rows = acc.shape[1]
    rest = rows - MAIN

    @pl.when(p == 0)
    def _():
        copies = [
            pltpu.make_async_copy(ref, amps.at[s], sems.at[s])
            for s, ref in enumerate((prev_hbm, own_hbm, next_hbm))
        ]
        for c in copies:
            c.start()
        for c in copies:
            c.wait()
        for o in range(OCC_DEV):
            packed = amps[1, o]
            acc[o] = lax.dot_general(packed, packed, CONTRACT_LAST, preferred_element_type=F32)

    low = lax.broadcasted_iota(jnp.int32, (1, 2 * rest), 1) < rest
    k = lax.rem(p, OCC_DEV)
    left = column(wanted(tab_ref[pl.ds(me * OCC_DEV + k - base, 1), :]), rows)
    right = column(
        wanted(tab_ref[pl.ds(partner[me * PAIR_DEV + p] - base, 1), :]), rows
    )
    held_rest, held_row = None, None
    for c in range(NCPL):
        m = near[p * NCPL + c]
        spot = m - (me - 1) * PAIR_DEV
        side, inner = spot // PAIR_DEV, lax.rem(spot, PAIR_DEV)
        slot, half = lax.rem(inner, OCC_DEV), inner // OCC_DEV
        i_m = (m // PAIR_DEV) * OCC_DEV + lax.rem(m, OCC_DEV) - base
        j_m = partner[m] - base
        scale = coef[p * NCPL + c]
        pick = lanes(left, tab_ref[pl.ds(i_m, 1), :])[:, :rows]
        main = amps[side, slot, :, pl.ds(pl.multiple_of(half * MAIN, MAIN), MAIN)]
        tail = amps[side, slot, :, 2 * MAIN :]
        got = jnp.dot(pick, main, preferred_element_type=F32) * scale
        rows_ref[:, c * MAIN : (c + 1) * MAIN] = got.astype(BF16)
        got = jnp.dot(pick, tail, preferred_element_type=F32) * scale
        got = jnp.where(half == c % 2, got, pltpu.roll(got, rest, 1))
        row = tab_ref[pl.ds(j_m, 1), :]
        cols_ref[:, c * MAIN : (c + 1) * MAIN] = lanes(right, row[:, :MAIN])
        row = row[:, MAIN:]
        if c % 2 == 0:
            held_rest, held_row = got, row
        else:
            at = NCPL * MAIN + (c // 2) * 2 * rest
            rows_ref[:, at : at + 2 * rest] = jnp.where(low, held_rest, got).astype(BF16)
            cols_ref[:, at : at + 2 * rest] = lanes(right, jnp.where(low, held_row, row))
    out_ref[0] = lax.dot_general(
        rows_ref[...], cols_ref[...], CONTRACT_LAST, preferred_element_type=F32
    )

    half = p // OCC_DEV
    for side in range(3):
        q = (me - 1 + side) * PAIR_DEV + p
        inside = (q >= 0) & (q < partner.shape[0])
        o = partner[jnp.clip(q, 0, partner.shape[0] - 1)] - me * OCC_DEV

        @pl.when(inside & (o >= 0) & (o < OCC_DEV))
        def _(side=side, o=o):
            main = amps[side, k, :, pl.ds(pl.multiple_of(half * MAIN, MAIN), MAIN)]
            tail = amps[side, k, :, 2 * MAIN :].astype(F32)
            tail = jnp.where(half == 0, tail, pltpu.roll(tail, rest, 1))
            whole = jnp.concatenate([main, tail[:, :rest].astype(BF16)], axis=1)
            acc[o] += lax.dot_general(
                whole, whole, (((0,), (0,)), ((), ())), preferred_element_type=F32
            )

    @pl.when(p == PAIR_DEV - 1)
    def _():
        dens_ref[...] = acc[...] / rows


def turn(order, stage, s):
    at = order[ORDER_START + stage] + s
    return order[jnp.minimum(at, PAIR_DEV - 1)]


def final_kernel(here, partner, order, *refs, base_of, stage):
    sources = len(CUTS[: stage + 2]) - 1
    tab_ref, gap_ref, picked_hbm, own_hbm = refs[:4]
    halos = refs[4 : 4 + 2 * sources]
    coupling_hbm, amp_hbm = refs[4 + 2 * sources : 6 + 2 * sources]
    rest_refs = refs[6 + 2 * sources :]
    if stage:
        before_ref, rest_refs = rest_refs[1], rest_refs[2:]
    new_hbm, energy_ref, block, picked, coupling, amps, new, sems, out_sems = rest_refs
    me = here[0]
    base = base_of(me)
    rows = new.shape[1]
    rest = rows - MAIN
    count = order[ORDER_COUNT + stage]

    def fetch(step, act):
        q = turn(order, stage, step)
        at = lax.rem(step, 2)
        spot = partner[me * PAIR_DEV + q] - (me - 1) * OCC_DEV
        slot, side = lax.rem(spot, OCC_DEV), spot // OCC_DEV
        act(pltpu.make_async_copy(picked_hbm.at[q], picked.at[at], sems.at[at, 1]))
        act(pltpu.make_async_copy(coupling_hbm.at[q], coupling.at[at], sems.at[at, 2]))
        act(pltpu.make_async_copy(amp_hbm.at[lax.rem(q, OCC_DEV)], amps.at[at], sems.at[at, 3]))

        def copy(ref, index):
            return pltpu.make_async_copy(ref.at[index], block.at[at], sems.at[at, 0])

        here_now = (side == 1) | (slot >= CUTS[sources])

        @pl.when(here_now)
        def _():
            act(copy(own_hbm, slot))

        for n in range(sources):
            for w, far in enumerate((0, 2)):

                @pl.when((side == far) & (slot >= CUTS[n]) & (slot < CUTS[n + 1]))
                def _(n=n, w=w):
                    act(copy(halos[2 * n + w], slot - CUTS[n]))

    def store(step):
        at = lax.rem(step, 2)
        return pltpu.make_async_copy(
            new.at[at], new_hbm.at[turn(order, stage, step)], out_sems.at[at]
        )

    fetch(0, lambda c: c.start())
    for q in range(PAIR_DEV):
        energy_ref[q] = before_ref[q] if stage else F32(0)

    @pl.loop(0, count)
    def _(s):
        @pl.when(s + 1 < count)
        def _():
            fetch(s + 1, lambda c: c.start())

        fetch(s, lambda c: c.wait())
        at = lax.rem(s, 2)

        @pl.when(s >= 2)
        def _():
            store(s - 2).wait()

        p = turn(order, stage, s)
        k, half = lax.rem(p, OCC_DEV), p // OCC_DEV
        first = me * OCC_DEV + k - base
        second = partner[me * PAIR_DEV + p] - base
        keep_left = column(tab_ref[pl.ds(first, 1), :], rows)[:, :1] >= 0
        gap_left = column(gap_ref[pl.ds(first, 1), :], rows)[:, :1]
        whole = lax.dot_general(picked[at], block[at], CONTRACT_LAST, preferred_element_type=F32)
        tail = amps[at, :, 2 * MAIN :].astype(F32)
        tail = jnp.where(half == 0, tail, pltpu.roll(tail, rest, 1))
        main = amps[at, :, pl.ds(pl.multiple_of(half * MAIN, MAIN), MAIN)].astype(F32)
        energy = F32(0)
        for start, size, amp in ((0, MAIN, main), (MAIN, rest, tail[:, :rest])):
            part = slice(start, start + size)
            keep = keep_left & (tab_ref[pl.ds(second, 1), :][:, part] >= 0)
            exchange = jnp.where(keep, whole[:, part], F32(0))
            denom = gap_left + gap_ref[pl.ds(second, 1), :][:, part]
            residual = exchange + denom * amp - coupling[at, :, part]
            new[at, :, part] = (amp - 0.5 * residual / denom).astype(BF16)
            energy += jnp.sum(exchange * amp)
        energy_ref[p] = energy / rows
        store(s).start()

    @pl.when(count >= 2)
    def _():
        store(count - 2).wait()

    store(count - 1).wait()


def whole_spec(shape):
    return pl.BlockSpec(shape, lambda *_: (0,) * len(shape))


def any_spec():
    return pl.BlockSpec(memory_space=pltpu.MemorySpace.HBM)


def call(kernel, prefetch, grid, ins, outs, scratch, args, flops, nbytes, aliases=None):
    return pl.pallas_call(
        kernel,
        out_shape=[s for s, _ in outs],
        grid_spec=pltpu.PrefetchScalarGridSpec(
            num_scalar_prefetch=len(prefetch),
            grid=grid,
            in_specs=ins,
            out_specs=[s for _, s in outs],
            scratch_shapes=scratch,
        ),
        cost_estimate=pl.CostEstimate(flops=flops, bytes_accessed=nbytes, transcendentals=0),
        compiler_params=pltpu.CompilerParams(vmem_limit_bytes=56 * 1024 * 1024),
        input_output_aliases=aliases or {},
    )(*prefetch, *args)


def neighbours(x):
    devices = lax.axis_size(AXES)
    up = [(i, i + 1) for i in range(devices - 1)]
    down = [(i + 1, i) for i in range(devices - 1)]
    before = lax.ppermute(x, AXES, up)
    after = lax.ppermute(x, AXES, down)
    return before, after


def local(
    blocks, aux_domain, pao_domain, pao_gap, amplitudes, pair_partner, coupling_list, coupling_coef
):
    here = lax.axis_index(AXES).astype(jnp.int32)
    norb, naux = aux_domain.shape
    npao = pao_domain.shape[1]
    span_aux, span_pao = 3 * OCC_DEV, 5 * OCC_DEV

    def base_aux(h):
        return jnp.clip((h - 1) * OCC_DEV, 0, norb - span_aux)

    def base_pao(h):
        return jnp.clip((h - 2) * OCC_DEV, 0, norb - span_pao)

    tab = lax.dynamic_slice(pao_domain, (base_pao(here), 0), (span_pao, npao))
    tab = jnp.concatenate([tab, tab[:, MAIN:]], axis=1)
    gap = lax.dynamic_slice(pao_gap, (base_pao(here), 0), (span_pao, npao))
    gap = jnp.concatenate([gap, gap[:, MAIN:]], axis=1)
    aux = lax.dynamic_slice(aux_domain, (base_aux(here), 0), (span_aux, naux))
    me = here[None]
    flat_near = coupling_list.reshape(-1)
    flat_coef = coupling_coef.reshape(-1)
    turned = jnp.swapaxes(blocks, 1, 2)
    packed_shape = (OCC_DEV, npao, 2 * npao)
    hbm = any_spec()
    sds = jax.ShapeDtypeStruct
    wide = tab.shape[1]

    halos = [neighbours(turned[CUTS[0] : CUTS[1]])]
    (packed,) = call(
        functools.partial(mask_kernel, base_of=base_pao),
        (me, pair_partner),
        (OCC_DEV,),
        [
            whole_spec((span_pao, wide)),
            pl.BlockSpec((1, npao, npao), lambda k, *_: (k, 0, 0)),
            pl.BlockSpec((1, npao, npao), lambda k, *_: (k + OCC_DEV, 0, 0)),
        ],
        [
            (
                sds(packed_shape, BF16),
                pl.BlockSpec((1, npao, 2 * npao), lambda k, *_: (k, 0, 0)),
            )
        ],
        [],
        (tab, amplitudes, amplitudes),
        1000,
        4_000_000,
    )
    amp_prev, amp_next = neighbours(packed)
    picked, order = call(
        functools.partial(align_kernel, base_of=base_aux),
        (me, pair_partner),
        (PAIR_DEV,),
        [
            whole_spec((span_aux, naux)),
            pl.BlockSpec((1, npao, naux), lambda p, *_: (lax.rem(p, OCC_DEV), 0, 0)),
        ],
        [
            (
                sds((PAIR_DEV, npao, naux), BF16),
                pl.BlockSpec((1, npao, naux), lambda p, *_: (p, 0, 0)),
            ),
            (
                sds((ORDER_SIZE,), jnp.int32),
                pl.BlockSpec(memory_space=pltpu.MemorySpace.SMEM),
            ),
        ],
        [pltpu.VMEM((naux, 128), jnp.int32)],
        (aux, turned),
        2 * PAIR_DEV * npao * naux * naux,
        8_000_000,
    )
    later, order = lax.optimization_barrier((turned[CUTS[1] : CUTS[2]], order))
    halos.append(neighbours(later))
    amp_prev, amp_next, later = lax.optimization_barrier((amp_prev, amp_next, turned[CUTS[2] :]))
    halos.append(neighbours(later))
    coupling, densities = call(
        functools.partial(coupling_kernel, base_of=base_pao),
        (me, pair_partner, flat_near, flat_coef),
        (PAIR_DEV,),
        [whole_spec((span_pao, wide)), hbm, hbm, hbm],
        [
            (
                sds((PAIR_DEV, npao, npao), F32),
                pl.BlockSpec((1, npao, npao), lambda p, *_: (p, 0, 0)),
            ),
            (sds((OCC_DEV, npao, npao), F32), whole_spec((OCC_DEV, npao, npao))),
        ],
        [
            pltpu.VMEM((3,) + packed_shape, BF16),
            pltpu.VMEM((npao, NCPL * npao), BF16),
            pltpu.VMEM((npao, NCPL * npao), BF16),
            pltpu.VMEM((OCC_DEV, npao, npao), F32),
            pltpu.SemaphoreType.DMA((3,)),
        ],
        (tab, amp_prev, packed, amp_next),
        2 * PAIR_DEV * (2 * NCPL + 2) * npao**3,
        12_000_000,
    )
    done = ()
    for stage in range(len(halos)):
        arrived = [x for pair in halos[: stage + 1] for x in pair]
        smem = pl.BlockSpec(memory_space=pltpu.MemorySpace.SMEM)
        vmem = pl.BlockSpec(memory_space=pltpu.MemorySpace.VMEM)
        inputs = (tab, gap, picked, turned, *arrived, coupling, packed)
        done = call(
            functools.partial(final_kernel, base_of=base_pao, stage=stage),
            (me, pair_partner, order),
            (),
            [vmem, vmem] + [hbm] * (len(inputs) - 2) + ([hbm, smem] if stage else []),
            [(sds((PAIR_DEV, npao, npao), BF16), hbm), (sds((PAIR_DEV,), F32), smem)],
            [
                pltpu.VMEM((2, npao, naux), BF16),
                pltpu.VMEM((2, npao, naux), BF16),
                pltpu.VMEM((2, npao, npao), F32),
                pltpu.VMEM((2, npao, 2 * npao), BF16),
                pltpu.VMEM((2, npao, npao), BF16),
                pltpu.SemaphoreType.DMA((2, 4)),
                pltpu.SemaphoreType.DMA((2,)),
            ],
            inputs + tuple(done),
            PAIR_DEV * npao * npao * naux,
            8_000_000,
            {3 + len(inputs): 0} if stage else None,
        )
    new_amps, energies = done
    return (new_amps, energies, densities)


def solution(mesh):
    return jax.shard_map(
        local,
        mesh=mesh,
        in_specs=(
            P(("orb", "pair"), None, None),
            P(),
            P(),
            P(),
            P(("orb", "pair"), None, None),
            P(),
            P(("orb", "pair"), None),
            P(("orb", "pair"), None),
        ),
        out_specs=(
            P(("orb", "pair"), None, None),
            P(("orb", "pair")),
            P(("orb", "pair"), None, None),
        ),
        check_vma=False,
    )
```

time: 502 us -> 126 us (0.25); the launches traced: 494 us -> 124 us
  local copies, waits for them, and re-layouts: 199 us -> 9.34 us
  waiting for transfers between devices: 101 us -> 20.1 us
  matrix products: 70.6 us -> 0 us
  Pallas kernels: 0 us -> 62 us
  loops' own time: 59.4 us -> 0 us
  other arithmetic: 33 us -> 1.43 us
    dynamic_update_slice x24 -> x0, local copies, waits for them, and re-layouts: 95.5 us -> none  [local(): lax.map(one_pair, (local_ids, amplitudes, coupling_list, coupling_coef))]
    ppermute x6 -> x8, waiting for transfers between devices: 101 us -> 20.1 us  [the longest x4 12.8 us: neighbours(): before = lax.ppermute(x, AXES, up)]
    dot_general x33 -> x0, matrix products: 70.6 us -> none  [the longest x8 30.6 us: pair_terms(): lax.dot_general(left_block, aligned, (((0,), (0,)), ((), ())), preferred_...]
    pallas_call x0 -> x6, Pallas kernels: none -> 62 us  [call(): pl.pallas_call(kernel, out_shape=[s for s, _ in outs], grid_spec=pltpu.Pr...]
    gather x33 -> x0, local copies, waits for them, and re-layouts: 60.3 us -> none  [the longest x8 27.5 us: one_pair(): near_amps = jnp.take(wide_amps, neighbours - pair_base, axis=0)]
    another operation x2 -> x0, loops' own time: 59.4 us -> none  [the longest x1 59.2 us: local(): lax.map(one_pair, (local_ids, amplitudes, coupling_list, coupling_coef))]
    dynamic_slice x32 -> x3, local copies, waits for them, and re-layouts: 23.1 us -> 3.63 us  [the longest x1 1.76 us: local(): gap = lax.dynamic_slice(pao_gap, (base_pao(here), 0), (span_pao, npao))]
    while x5 -> x0, local copies, waits for them, and re-layouts: 16.3 us -> none  [local(): lax.map(one_pair, (local_ids, amplitudes, coupling_list, coupling_coef))]
  transfers between devices with their start and end apart: 6 -> 8, of which waited for: 4 -> 4; matrix products, arithmetic and copies ran while one was open for 3% -> 6% of each run, Pallas kernels for 0% -> 42%
where the time goes in v1:
time: 126 us; the launch traced here: 124 us
  Pallas kernels  62 us (49%)
  starting transfers between devices  30.4 us (24%)
  waiting for transfers between devices  20.1 us (16%)
  local copies, waits for them, and re-layouts  9.34 us (7%)
  other arithmetic  1.43 us (1%)
    pallas_call x6, Pallas kernels, call(): pl.pallas_call(kernel, out_shape=[s for s, _ in outs], grid_spec=pltpu.Pr...  62 us
    ppermute x4, starting transfers between devices, neighbours(): after = lax.ppermute(x, AXES, down)  20.8 us
    ppermute x4, waiting for transfers between devices, neighbours(): before = lax.ppermute(x, AXES, up)  12.8 us
    ppermute x4, starting transfers between devices, neighbours(): before = lax.ppermute(x, AXES, up)  9.65 us
    ppermute x4, waiting for transfers between devices, neighbours(): after = lax.ppermute(x, AXES, down)  7.28 us
  transfers between devices with their start and end apart: 8, of which 4 were waited for; matrix products, arithmetic and copies ran while one was open for 6% of the time, Pallas kernels for 42%

profile of v1, /device:TPU:96, one launch (start us, length us, event | category | flops | bytes accessed | tf_op | source)
XLA Modules:
  0.0 124.1 jit_solution(6922251891181398979)
XLA Ops:
  0.6 0.0 copy-start
  0.7 1.2 constant_dynamic-slice_fusion.1
  1.9 0.1 copy.21
  2.0 0.7 pad_add_fusion.tab_ref.refs_0_
  2.7 0.0 copy-start.1
  2.7 5.2 %shard_map.104.own_hbm.refs_7_.refs_9_.refs_11_ = bf16[4,320,640]{2,1,0:T(8,128)(2,1)} custom-call(s32[1]{0:T(128)} %bitcast.here, s32[1024]{0:T(1024)} %partner.11, s32[20,384]{1,0:T(8,128)} %pad_add_fusion.tab_ref.refs_0_, bf16[8,320,320]{2,1,0:T(8,128)(2,1)} %high_ref.1, bf16[8,320,320]{2,1,0:T(8,128)(2,1)} %high_ref.1), custom_call_target="tpu_custom_call" | custom-call | flops 1000 | bytes 4000000 | tf_op jit(solution)/shard_map/pallas_call | solution.py:296
  7.9 6.4 %collective-permute-start.5 = (bf16[4,320,640]{2,1,0:T(8,128)(2,1)}, bf16[4,320,640]{2,1,0:T(8,128)(2,1)}, u32[]{:S(2)}, u32[]{:S(2)}) collective-permute-start(bf16[4,320,640]{2,1,0:T(8,128)(2,1)} %shard_map.104.own_hbm.refs_7_.refs_9_.refs_11_), channel_id=1, source_target_pairs={{1,0},{2,1},{3,2},{4,3},{5,4},{6,5},{7,6},{8,7},{9,8},{10,9},{11,1... | collective-permute-start | bytes 4915208 | tf_op jit(solution)/shard_map/ppermute | solution.py:317
  14.3 1.9 %collective-permute-start.4 = (bf16[4,320,640]{2,1,0:T(8,128)(2,1)}, bf16[4,320,640]{2,1,0:T(8,128)(2,1)}, u32[]{:S(2)}, u32[]{:S(2)}) collective-permute-start(bf16[4,320,640]{2,1,0:T(8,128)(2,1)} %shard_map.104.own_hbm.refs_7_.refs_9_.refs_11_), channel_id=1, source_target_pairs={{0,1},{1,2},{2,3},{3,4},{4,5},{5,6},{6,7},{7,8},{8,9},{9,10},{10,1... | collective-permute-start | bytes 4915208 | tf_op jit(solution)/shard_map/ppermute | solution.py:316
  16.2 0.0 copy-done.1
  16.2 1.1 fusion
  17.4 7.8 %collective-permute-start.1 = (bf16[1,320,1024]{2,1,0:T(8,128)(2,1)}, bf16[1,320,1024]{2,1,0:T(8,128)(2,1)S(1)}, u32[]{:S(2)}, u32[]{:S(2)}) collective-permute-start(bf16[1,320,1024]{2,1,0:T(8,128)(2,1)} %get-tuple-element.34), channel_id=1, source_target_pairs={{1,0},{2,1},{3,2},{4,3},{5,4},{6,5},{7,6},{8,7},{9,8},{10,9},{11,1... | collective-permute-start | bytes 1966088 | tf_op jit(solution)/shard_map/ppermute | solution.py:317
  25.3 0.0 copy-done
  25.3 0.6 constant_dynamic-slice_fusion.2.aux_ref
  25.9 11.8 %shard_map.103 = (bf16[8,320,1024]{2,1,0:T(8,128)(2,1)}, s32[32]{0:T(128)}) custom-call(s32[1]{0:T(128)} %bitcast.here, s32[1024]{0:T(1024)} %partner.11, s32[12,1024]{1,0:T(8,128)} %constant_dynamic-slice_fusion.2.aux_ref, bf16[4,320,1024]{2,1,0:T(8,128)(2,1)} %bitcast.2), custom_call_target="tpu_custom_call" | custom-call | flops 5368709120 | bytes 8000000 | tf_op jit(solution)/shard_map/pallas_call | solution.py:296
  37.7 0.0 copy-done.2
  37.7 0.0 copy-start.5
  37.7 0.0 copy-start.6
  37.7 1.2 slice.20
  38.9 1.9 %collective-permute-start.3 = (bf16[2,320,1024]{2,1,0:T(8,128)(2,1)}, bf16[2,320,1024]{2,1,0:T(8,128)(2,1)}, u32[]{:S(2)}, u32[]{:S(2)}) collective-permute-start(bf16[2,320,1024]{2,1,0:T(8,128)(2,1)} %slice.20), channel_id=1, source_target_pairs={{1,0},{2,1},{3,2},{4,3},{5,4},{6,5},{7,6},{8,7},{9,8},{10,9},{11,1... | collective-permute-start | bytes 3932168 | tf_op jit(solution)/shard_map/ppermute | solution.py:317
  40.8 3.9 %collective-permute-start.2 = (bf16[2,320,1024]{2,1,0:T(8,128)(2,1)}, bf16[2,320,1024]{2,1,0:T(8,128)(2,1)}, u32[]{:S(2)}, u32[]{:S(2)}) collective-permute-start(bf16[2,320,1024]{2,1,0:T(8,128)(2,1)} %slice.20), channel_id=1, source_target_pairs={{0,1},{1,2},{2,3},{3,4},{4,5},{5,6},{6,7},{7,8},{8,9},{9,10},{10,1... | collective-permute-start | bytes 3932168 | tf_op jit(solution)/shard_map/ppermute | solution.py:316
  44.7 6.0 %collective-permute-done.5.next_hbm = bf16[4,320,640]{2,1,0:T(8,128)(2,1)} collective-permute-done((bf16[4,320,640]{2,1,0:T(8,128)(2,1)}, bf16[4,320,640]{2,1,0:T(8,128)(2,1)}, u32[]{:S(2)}, u32[]{:S(2)}) %collective-permute-start.5) | collective-permute-done | bytes 1638432 | tf_op jit(solution)/shard_map/ppermute | solution.py:317
  50.7 1.9 %collective-permute-start = (bf16[1,320,1024]{2,1,0:T(8,128)(2,1)}, bf16[1,320,1024]{2,1,0:T(8,128)(2,1)S(1)}, u32[]{:S(2)}, u32[]{:S(2)}) collective-permute-start(bf16[1,320,1024]{2,1,0:T(8,128)(2,1)} %get-tuple-element.34), channel_id=1, source_target_pairs={{0,1},{1,2},{2,3},{3,4},{4,5},{5,6},{6,7},{7,8},{8,9},{9,10},{10,1... | collective-permute-start | bytes 1966088 | tf_op jit(solution)/shard_map/ppermute | solution.py:316
  52.6 1.8 %constant_dynamic-slice_fusion = f32[20,320]{0,1:T(8,128)} fusion(f32[512,320]{0,1:T(8,128)} %param.11, s32[]{:T(128)S(6)} %min.9), kind=kLoop, calls=%fused_computation.2 | loop fusion | bytes 51204 | tf_op jit(solution)/shard_map/dynamic_slice | solution.py:337
  54.4 1.0 copy.22
  55.4 3.4 %collective-permute-done.4.prev_hbm = bf16[4,320,640]{2,1,0:T(8,128)(2,1)} collective-permute-done((bf16[4,320,640]{2,1,0:T(8,128)(2,1)}, bf16[4,320,640]{2,1,0:T(8,128)(2,1)}, u32[]{:S(2)}, u32[]{:S(2)}) %collective-permute-start.4) | collective-permute-done | bytes 1638432 | tf_op jit(solution)/shard_map/ppermute | solution.py:316
  58.8 4.6 %collective-permute-start.7 = (bf16[1,320,1024]{2,1,0:T(8,128)(2,1)}, bf16[1,320,1024]{2,1,0:T(8,128)(2,1)}, u32[]{:S(2)}, u32[]{:S(2)}) collective-permute-start(bf16[1,320,1024]{2,1,0:T(8,128)(2,1)} %get-tuple-element.22), channel_id=1, source_target_pairs={{1,0},{2,1},{3,2},{4,3},{5,4},{6,5},{7,6},{8,7},{9,8},{10,9},{11,1... | collective-permute-start | bytes 1966088 | tf_op jit(solution)/shard_map/ppermute | solution.py:317
  63.4 1.3 %collective-permute-done.1.refs_5_ = bf16[1,320,1024]{2,1,0:T(8,128)(2,1)S(1)} collective-permute-done((bf16[1,320,1024]{2,1,0:T(8,128)(2,1)}, bf16[1,320,1024]{2,1,0:T(8,128)(2,1)S(1)}, u32[]{:S(2)}, u32[]{:S(2)}) %collective-permute-start.1) | collective-permute-done | bytes 655392 | tf_op jit(solution)/shard_map/ppermute | solution.py:317
  64.7 0.0 copy-start.3
  64.7 1.9 %collective-permute-start.6 = (bf16[1,320,1024]{2,1,0:T(8,128)(2,1)}, bf16[1,320,1024]{2,1,0:T(8,128)(2,1)}, u32[]{:S(2)}, u32[]{:S(2)}) collective-permute-start(bf16[1,320,1024]{2,1,0:T(8,128)(2,1)} %get-tuple-element.22), channel_id=1, source_target_pairs={{0,1},{1,2},{2,3},{3,4},{4,5},{5,6},{6,7},{7,8},{8,9},{9,10},{10,1... | collective-permute-start | bytes 1966088 | tf_op jit(solution)/shard_map/ppermute | solution.py:316
  66.7 0.7 pad_maximum_fusion.refs_1_
  67.3 0.0 copy-done.5
  67.4 0.1 copy.19
  67.4 0.6 reshape.12.near
  68.0 0.0 copy-done.6
  68.0 0.1 copy.20
  68.1 0.7 reshape.13.coef
  68.8 22.7 %shard_map.105 = (f32[8,320,320]{2,1,0:T(8,128)}, f32[4,320,320]{2,1,0:T(8,128)}) custom-call(s32[1]{0:T(128)} %bitcast.here, s32[1024]{0:T(1024)} %partner.11, s32[32]{0:T(128)} %reshape.12.near, f32[32]{0:T(128)} %reshape.13.coef, s32[20,384]{1,0:T(8,128)} %pad_add_fusion.tab_ref.refs_0_, bf16[4,320,640]{2,1,0:T(8,128)(2,1)} %collective-permute-done.4.prev_hbm, ...), custom_call_target="tpu_custom_call" | custom-call | flops 5242880000 | bytes 12000000 | tf_op jit(solution)/shard_map/pallas_call | solution.py:296
  91.5 0.0 copy-done.3
  91.5 9.4 %collective-permute-done.refs_4_ = bf16[1,320,1024]{2,1,0:T(8,128)(2,1)S(1)} collective-permute-done((bf16[1,320,1024]{2,1,0:T(8,128)(2,1)}, bf16[1,320,1024]{2,1,0:T(8,128)(2,1)S(1)}, u32[]{:S(2)}, u32[]{:S(2)}) %collective-permute-start) | collective-permute-done | bytes 655392 | tf_op jit(solution)/shard_map/ppermute | solution.py:316
  100.9 0.0 copy-start.4
  100.9 0.8 copy-done.4
  101.7 12.2 %shard_map.106 = (bf16[8,320,320]{2,1,0:T(8,128)(2,1)}, f32[8]{0:T(128)}) custom-call(s32[1]{0:T(128)} %bitcast.here, s32[1024]{0:T(1024)} %partner.11, s32[32]{0:T(128)} %get-tuple-element.19.order, s32[20,384]{1,0:T(8,128)} %pad_add_fusion.tab_ref.refs_0_, f32[20,384]{1,0:T(8,128)} %pad_maximum_fusion.refs_1_, ...), custom_call_target="tpu_custom_call" | custom-call | flops 838860800 | bytes 8000000 | tf_op jit(solution)/shard_map/pallas_call | solution.py:296
  113.9 0.0 collective-permute-done.3.refs_7_
  113.9 0.0 collective-permute-done.2.refs_6_
  113.9 5.1 %shard_map.107 = (bf16[8,320,320]{2,1,0:T(8,128)(2,1)}, f32[8]{0:T(128)}) custom-call(s32[1]{0:T(128)} %bitcast.here, s32[1024]{0:T(1024)} %partner.11, s32[32]{0:T(128)} %get-tuple-element.19.order, s32[20,384]{1,0:T(8,128)} %pad_add_fusion.tab_ref.refs_0_, f32[20,384]{1,0:T(8,128)} %pad_maximum_fusion.refs_1_, ...), custom_call_target="tpu_custom_call", output_to_operand_aliasing={{0}: (13, {})} | custom-call | flops 838860800 | bytes 8000000 | tf_op jit(solution)/shard_map/pallas_call | solution.py:296
  119.0 0.0 collective-permute-done.7.refs_9_
  119.0 0.0 collective-permute-done.6.refs_8_
  119.0 5.1 %shard_map.108 = (bf16[8,320,320]{2,1,0:T(8,128)(2,1)}, f32[8]{0:T(128)}) custom-call(s32[1]{0:T(128)} %bitcast.here, s32[1024]{0:T(1024)} %partner.11, s32[32]{0:T(128)} %get-tuple-element.19.order, s32[20,384]{1,0:T(8,128)} %pad_add_fusion.tab_ref.refs_0_, f32[20,384]{1,0:T(8,128)} %pad_maximum_fusion.refs_1_, ...), custom_call_target="tpu_custom_call", output_to_operand_aliasing={{0}: (15, {})} | custom-call | flops 838860800 | bytes 8000000 | tf_op jit(solution)/shard_map/pallas_call | solution.py:296
  (3 shorter events, 0.0 us)
Async XLA Ops:
  0.6 24.6 %copy-start = (s32[512,1024]{1,0:T(8,128)S(1)}, s32[512,1024]{1,0:T(8,128)}, u32[]{:S(2)}) copy-start(s32[512,1024]{1,0:T(8,128)} %param.9) | copy-start | bytes 6291460
  2.7 13.5 %copy-start.1 = (bf16[4,1024,320]{1,2,0:T(8,128)(2,1)S(1)}, bf16[4,1024,320]{1,2,0:T(8,128)(2,1)}, u32[]{:S(2)}) copy-start(bf16[4,1024,320]{1,2,0:T(8,128)(2,1)} %param.8) | copy-start | bytes 7864324
  7.9 42.8 %collective-permute-start.5 = (bf16[4,320,640]{2,1,0:T(8,128)(2,1)}, bf16[4,320,640]{2,1,0:T(8,128)(2,1)}, u32[]{:S(2)}, u32[]{:S(2)}) collective-permute-start(bf16[4,320,640]{2,1,0:T(8,128)(2,1)} %shard_map.104.own_hbm.refs_7_.refs_9_.refs_11_), channel_id=1, source_target_pairs={{1,0},{2,1},{3,2},{4,3},{5,4},{6,5},{7,6},{8,7},{9,8},{10,9},{11,1... | collective-permute-start | bytes 4915208 | tf_op jit(solution)/shard_map/ppermute | solution.py:317
  14.3 44.5 %collective-permute-start.4 = (bf16[4,320,640]{2,1,0:T(8,128)(2,1)}, bf16[4,320,640]{2,1,0:T(8,128)(2,1)}, u32[]{:S(2)}, u32[]{:S(2)}) collective-permute-start(bf16[4,320,640]{2,1,0:T(8,128)(2,1)} %shard_map.104.own_hbm.refs_7_.refs_9_.refs_11_), channel_id=1, source_target_pairs={{0,1},{1,2},{2,3},{3,4},{4,5},{5,6},{6,7},{7,8},{8,9},{9,10},{10,1... | collective-permute-start | bytes 4915208 | tf_op jit(solution)/shard_map/ppermute | solution.py:316
  17.4 47.4 %collective-permute-start.1 = (bf16[1,320,1024]{2,1,0:T(8,128)(2,1)}, bf16[1,320,1024]{2,1,0:T(8,128)(2,1)S(1)}, u32[]{:S(2)}, u32[]{:S(2)}) collective-permute-start(bf16[1,320,1024]{2,1,0:T(8,128)(2,1)} %get-tuple-element.34), channel_id=1, source_target_pairs={{1,0},{2,1},{3,2},{4,3},{5,4},{6,5},{7,6},{8,7},{9,8},{10,9},{11,1... | collective-permute-start | bytes 1966088 | tf_op jit(solution)/shard_map/ppermute | solution.py:317
  25.9 11.8 %copy-start.2 = (bf16[4,1024,320]{1,2,0:T(8,128)(2,1)S(1)}, bf16[4,1024,320]{1,2,0:T(8,128)(2,1)}, u32[]{:S(2)}) copy-start(bf16[4,1024,320]{1,2,0:T(8,128)(2,1)} %param.8) | copy-start | bytes 7864324
  37.7 29.7 %copy-start.5 = (s32[8,4]{0,1:T(4,128)S(1)}, s32[8,4]{0,1:T(4,128)}, u32[]{:S(2)}) copy-start(s32[8,4]{0,1:T(4,128)} %param.14) | copy-start | bytes 388
  37.7 30.3 %copy-start.6 = (f32[8,4]{0,1:T(4,128)S(1)}, f32[8,4]{0,1:T(4,128)}, u32[]{:S(2)}) copy-start(f32[8,4]{0,1:T(4,128)} %param.15) | copy-start | bytes 388
  38.9 75.0 %collective-permute-start.3 = (bf16[2,320,1024]{2,1,0:T(8,128)(2,1)}, bf16[2,320,1024]{2,1,0:T(8,128)(2,1)}, u32[]{:S(2)}, u32[]{:S(2)}) collective-permute-start(bf16[2,320,1024]{2,1,0:T(8,128)(2,1)} %slice.20), channel_id=1, source_target_pairs={{1,0},{2,1},{3,2},{4,3},{5,4},{6,5},{7,6},{8,7},{9,8},{10,9},{11,1... | collective-permute-start | bytes 3932168 | tf_op jit(solution)/shard_map/ppermute | solution.py:317
  40.8 73.1 %collective-permute-start.2 = (bf16[2,320,1024]{2,1,0:T(8,128)(2,1)}, bf16[2,320,1024]{2,1,0:T(8,128)(2,1)}, u32[]{:S(2)}, u32[]{:S(2)}) collective-permute-start(bf16[2,320,1024]{2,1,0:T(8,128)(2,1)} %slice.20), channel_id=1, source_target_pairs={{0,1},{1,2},{2,3},{3,4},{4,5},{5,6},{6,7},{7,8},{8,9},{9,10},{10,1... | collective-permute-start | bytes 3932168 | tf_op jit(solution)/shard_map/ppermute | solution.py:316
  50.7 50.2 %collective-permute-start = (bf16[1,320,1024]{2,1,0:T(8,128)(2,1)}, bf16[1,320,1024]{2,1,0:T(8,128)(2,1)S(1)}, u32[]{:S(2)}, u32[]{:S(2)}) collective-permute-start(bf16[1,320,1024]{2,1,0:T(8,128)(2,1)} %get-tuple-element.34), channel_id=1, source_target_pairs={{0,1},{1,2},{2,3},{3,4},{4,5},{5,6},{6,7},{7,8},{8,9},{9,10},{10,1... | collective-permute-start | bytes 1966088 | tf_op jit(solution)/shard_map/ppermute | solution.py:316
  58.8 60.2 %collective-permute-start.7 = (bf16[1,320,1024]{2,1,0:T(8,128)(2,1)}, bf16[1,320,1024]{2,1,0:T(8,128)(2,1)}, u32[]{:S(2)}, u32[]{:S(2)}) collective-permute-start(bf16[1,320,1024]{2,1,0:T(8,128)(2,1)} %get-tuple-element.22), channel_id=1, source_target_pairs={{1,0},{2,1},{3,2},{4,3},{5,4},{6,5},{7,6},{8,7},{9,8},{10,9},{11,1... | collective-permute-start | bytes 1966088 | tf_op jit(solution)/shard_map/ppermute | solution.py:317
  64.7 26.8 %copy-start.3 = (bf16[1,320,1024]{2,1,0:T(8,128)(2,1)}, bf16[1,320,1024]{2,1,0:T(8,128)(2,1)S(1)}, u32[]{:S(2)}) copy-start(bf16[1,320,1024]{2,1,0:T(8,128)(2,1)S(1)} %collective-permute-done.1.refs_5_) | copy-start | bytes 1966084
  64.7 54.3 %collective-permute-start.6 = (bf16[1,320,1024]{2,1,0:T(8,128)(2,1)}, bf16[1,320,1024]{2,1,0:T(8,128)(2,1)}, u32[]{:S(2)}, u32[]{:S(2)}) collective-permute-start(bf16[1,320,1024]{2,1,0:T(8,128)(2,1)} %get-tuple-element.22), channel_id=1, source_target_pairs={{0,1},{1,2},{2,3},{3,4},{4,5},{5,6},{6,7},{7,8},{8,9},{9,10},{10,1... | collective-permute-start | bytes 1966088 | tf_op jit(solution)/shard_map/ppermute | solution.py:316
  100.9 0.8 copy-start.4

commit v2 on v0

v2 whole, which is shorter than its diff:
```python
import functools

import jax
import jax.numpy as jnp
from jax import lax
from jax.experimental import pallas as pl
from jax.experimental.pallas import tpu as pltpu
from jax.sharding import PartitionSpec as P

OCC_DEV = 4
PAIR_DEV = 8
NCPL = 4
F32 = jnp.float32
BF16 = jnp.bfloat16
MAIN = 256
LANE = 128
MESH = pl.DeviceIdType.MESH
CONTRACT_LAST = (((1,), (1,)), ((), ()))
CONTRACT_FIRST = (((0,), (0,)), ((), ()))
CUTS = ((0, 256), (256, 768), (768, 1024))


def column(row, rows):
    wide = jnp.broadcast_to(row, (LANE, row.shape[1]))
    return wide.T[:rows]


def wanted(row):
    return jnp.where(row < 0, -2, row)


def lanes(col, row):
    pieces = [
        jnp.where(col == row[:, at : at + LANE], F32(1), F32(0)).astype(BF16)
        for at in range(0, row.shape[1], LANE)
    ]
    return pieces[0] if len(pieces) == 1 else jnp.concatenate(pieces, axis=1)


def wrapped(index, length):
    return lax.rem(lax.rem(index, length) + length, length)


def dot(a, b, dims=(((1,), (0,)), ((), ()))):
    return lax.dot_general(a, b, dims, preferred_element_type=F32)


def kernel(
    devices,
    partner,
    near,
    coef,
    blocks_hbm,
    aux_hbm,
    pao_hbm,
    gap_hbm,
    amps_hbm,
    new_hbm,
    energy_ref,
    dens_hbm,
    own,
    aux,
    pao_window,
    gap_window,
    raw,
    tab,
    gap,
    amps,
    picked,
    part0,
    part1,
    part2,
    exch,
    scale_ref,
    base_ref,
    rows_ref,
    cols_ref,
    acc,
    new,
    local_sems,
    send_sems,
    recv_sems,
    out_sems,
):
    pairs_axis = lax.axis_size("pair")
    me = lax.axis_index("orb") * pairs_axis + lax.axis_index("pair")
    npao, naux = own.shape[1:]
    norb = aux_hbm.shape[0]
    rest = npao - MAIN
    parts = (part0, part1, part2)
    has = (me > 0, me < devices - 1)
    peers = tuple(
        (lax.div(at, pairs_axis), lax.rem(at, pairs_axis))
        for at in (lax.rem(me + devices - 1, devices), lax.rem(me + 1, devices))
    )

    groups = norb // 8
    group = me // 2
    aux_start = (group - 1) * 8
    loads = [
        pltpu.make_async_copy(src, dst, local_sems.at[n])
        for n, (src, dst) in enumerate(
            (
                (pao_hbm, pao_window),
                (amps_hbm, raw),
                (blocks_hbm, own),
                (gap_hbm, gap_window),
                (blocks_hbm.at[:, :, CUTS[0][0] : CUTS[0][1]], part0.at[1]),
                (blocks_hbm.at[:, :, CUTS[1][0] : CUTS[1][1]], part1.at[1]),
                (blocks_hbm.at[:, :, CUTS[2][0] : CUTS[2][1]], part2.at[1]),
                *[
                    (
                        aux_hbm.at[pl.ds(lax.rem(group + groups - 1 + g, groups) * 8, 8)],
                        aux.at[8 * g : 8 * g + 8],
                    )
                    for g in range(3)
                ],
            )
        )
    ]
    for copy in loads:
        copy.start()

    barrier = pltpu.get_barrier_semaphore()
    for side in range(2):

        @pl.when(has[side])
        def _(side=side):
            pl.semaphore_signal(barrier, inc=1, device_id=peers[side], device_id_type=MESH)

    inner = jnp.logical_and(*has)

    @pl.when(inner)
    def _():
        pl.semaphore_wait(barrier, 2)

    @pl.when(jnp.logical_not(inner))
    def _():
        pl.semaphore_wait(barrier, 1)

    def remote(n, side):
        if n < len(CUTS):
            src = blocks_hbm.at[:, :, CUTS[n][0] : CUTS[n][1]]
            dst = parts[n].at[2 - 2 * side]
        else:
            src, dst = amps.at[1], amps.at[2 - 2 * side]
        return pltpu.make_async_remote_copy(
            src_ref=src,
            dst_ref=dst,
            send_sem=send_sems.at[n, side],
            recv_sem=recv_sems.at[n, side],
            device_id=peers[side],
            device_id_type=MESH,
        )

    def start(n):
        for side in range(2):

            @pl.when(has[side])
            def _(side=side):
                remote(n, side).start()

    def sent(n):
        for side in range(2):

            @pl.when(has[side])
            def _(side=side):
                remote(n, side).wait_send()

    def arrived(n):
        for side in range(2):

            @pl.when(has[1 - side])
            def _(side=side):
                remote(n, side).wait_recv()

    start(0)

    def rows_of(window):
        x = window[...]
        return jnp.concatenate([x, x[MAIN:]], axis=0).T

    loads[0].wait()
    tab[...] = rows_of(pao_window)
    loads[1].wait()
    first = me * OCC_DEV

    @pl.loop(0, OCC_DEV)
    def _(k):
        left = column(tab[pl.ds(first + k, 1), :], npao)[:, :1] >= 0
        tails = []
        for n in range(2):
            p = k + n * OCC_DEV
            at = partner[me * PAIR_DEV + p]
            keep = left & (tab[pl.ds(at, 1), :] >= 0)[:, :npao]
            amp = jnp.where(keep, raw[p].astype(F32), F32(0))
            amps[1, k, :, n * MAIN : (n + 1) * MAIN] = amp[:, :MAIN].astype(BF16)
            tails.append(amp[:, MAIN:])
        amps[1, k, :, 2 * MAIN :] = jnp.concatenate(tails, axis=1).astype(BF16)

    loads[3].wait()
    gap[...] = rows_of(gap_window)
    for side in range(2):

        @pl.when(jnp.logical_not(has[side]))
        def _(side=side):
            amps[2 * side] = jnp.zeros_like(amps[2 * side])

    loads[2].wait()
    for g in range(3):
        loads[7 + g].wait()

    def align(p):
        k = lax.rem(p, OCC_DEV)
        col = column(aux[pl.ds(me * OCC_DEV + k - aux_start, 1), :], naux)
        second = wrapped(partner[me * PAIR_DEV + p] - aux_start, aux.shape[0])
        present = aux[pl.ds(second, 1), :]
        for at in range(0, naux, MAIN):
            pick = lanes(col, present[:, at : at + MAIN])
            picked[p, :, at : at + MAIN] = dot(own[k], pick).astype(BF16)

    pl.loop(0, 1)(align)
    start(3)
    pl.loop(1, PAIR_DEV)(align)

    def amp_of(side, p):
        k, half = lax.rem(p, OCC_DEV), lax.div(p, OCC_DEV)
        main = amps[side, k, :, pl.ds(pl.multiple_of(half * MAIN, MAIN), MAIN)]
        tail = amps[side, k, :, 2 * MAIN :].astype(F32)
        tail = jnp.where(half == 0, tail, pltpu.roll(tail, rest, 1))
        return main, tail[:, :rest]

    def right_terms(side):
        @pl.loop(0, PAIR_DEV)
        def _(p):
            q = lax.rem((me + devices - 1 + side) * PAIR_DEV + p, devices * PAIR_DEV)
            target = partner[q] - me * OCC_DEV
            main, tail = amp_of(side, p)
            whole = jnp.concatenate([main, tail.astype(BF16)], axis=1)
            term = dot(whole, whole, CONTRACT_FIRST)
            for o in range(OCC_DEV):
                acc[o] += jnp.where(target == o, F32(1), F32(0)) * term

    for o in range(OCC_DEV):
        packed = amps[1, o]
        acc[o] = dot(packed, packed, CONTRACT_LAST)
    right_terms(1)

    def block_of(part, p):
        spot = wrapped(partner[me * PAIR_DEV + p] - (me - 1) * OCC_DEV, 3 * OCC_DEV)
        return part[lax.div(spot, OCC_DEV), lax.rem(spot, OCC_DEV)]

    def exchange_term(n, p):
        lo, hi = CUTS[n]
        return dot(picked[p, :, lo:hi], block_of(parts[n], p), CONTRACT_LAST)

    loads[4].wait()
    arrived(0)

    @pl.loop(0, PAIR_DEV)
    def _(p):
        exch[p] = exchange_term(0, p)

    sent(3)
    start(1)
    arrived(3)
    low = lax.broadcasted_iota(jnp.int32, (1, 2 * rest), 1) < rest

    @pl.loop(0, PAIR_DEV)
    def _(p):
        i_row = me * OCC_DEV + lax.rem(p, OCC_DEV)
        j_row = partner[me * PAIR_DEV + p]
        left = column(wanted(tab[pl.ds(i_row, 1), :]), npao)
        right = column(wanted(tab[pl.ds(j_row, 1), :]), npao)
        held_rest, held_row = None, None
        for c in range(NCPL):
            m = near[c, p]
            spot = wrapped(m - (me - 1) * PAIR_DEV, 3 * PAIR_DEV)
            side, inner = lax.div(spot, PAIR_DEV), lax.rem(spot, PAIR_DEV)
            slot, half = lax.rem(inner, OCC_DEV), lax.div(inner, OCC_DEV)
            i_m = lax.div(m, PAIR_DEV) * OCC_DEV + slot
            j_m = partner[m]
            scale = coef[c, p]
            pick = lanes(left, tab[pl.ds(i_m, 1), :])[:, :npao]
            both = amps[side, slot]
            main = jnp.where(half == 0, both[:, :MAIN], both[:, MAIN : 2 * MAIN])
            tail = both[:, 2 * MAIN :]
            rows_ref[:, c * MAIN : (c + 1) * MAIN] = (dot(pick, main) * scale).astype(BF16)
            got = dot(pick, tail) * scale
            got = jnp.where(half == c % 2, got, pltpu.roll(got, rest, 1))
            row = tab[pl.ds(j_m, 1), :]
            cols_ref[:, c * MAIN : (c + 1) * MAIN] = lanes(right, row[:, :MAIN])
            row = row[:, MAIN:]
            if c % 2 == 0:
                held_rest, held_row = got, row
            else:
                at = NCPL * MAIN + (c // 2) * 2 * rest
                rows_ref[:, at : at + 2 * rest] = jnp.where(low, held_rest, got).astype(BF16)
                cols_ref[:, at : at + 2 * rest] = lanes(right, jnp.where(low, held_row, row))
        coupling = dot(rows_ref[...], cols_ref[...], CONTRACT_LAST)
        gap_left = column(gap[pl.ds(i_row, 1), :], npao)[:, :1]
        gap_right = gap[pl.ds(j_row, 1), :]
        keep_right = tab[pl.ds(j_row, 1), :] >= 0
        main, tail = amp_of(1, p)
        for lo, hi, amp in ((0, MAIN, main.astype(F32)), (MAIN, npao, tail)):
            keep = (left[:, :1] >= 0) & keep_right[:, lo:hi]
            denom = gap_left + gap_right[:, lo:hi]
            half_inverse = 0.5 / denom
            scale_ref[p, :, lo:hi] = jnp.where(keep, half_inverse, F32(0))
            base_ref[p, :, lo:hi] = amp - (denom * amp - coupling[:, lo:hi]) * half_inverse

    start(2)
    right_terms(0)
    right_terms(2)
    acc[...] = acc[...] / npao
    dens_out = pltpu.make_async_copy(acc, dens_hbm, out_sems.at[PAIR_DEV])
    dens_out.start()

    loads[5].wait()
    arrived(1)

    @pl.loop(0, PAIR_DEV)
    def _(p):
        exch[p] += exchange_term(1, p)

    loads[6].wait()
    arrived(2)

    @pl.loop(0, PAIR_DEV)
    def _(p):
        whole = exch[p] + exchange_term(2, p)
        main, tail = amp_of(1, p)
        new[p] = (base_ref[p] - scale_ref[p] * whole).astype(BF16)
        energy = jnp.sum(whole[:, :MAIN] * main.astype(F32)) + jnp.sum(whole[:, MAIN:] * tail)
        energy_ref[p] = energy / npao
        pltpu.make_async_copy(new.at[p], new_hbm.at[p], out_sems.at[p]).start()

    for p in range(PAIR_DEV):
        pltpu.make_async_copy(new.at[p], new_hbm.at[p], out_sems.at[p]).wait()
    dens_out.wait()
    for n in range(3):
        sent(n)


def local(
    blocks, aux_domain, pao_domain, pao_gap, amplitudes, pair_partner, coupling_list, coupling_coef
):
    devices = lax.axis_size(("orb", "pair"))
    naux, npao = blocks.shape[1:]
    norb = aux_domain.shape[0]
    hbm = pl.BlockSpec(memory_space=pltpu.MemorySpace.HBM)
    smem = pl.BlockSpec(memory_space=pltpu.MemorySpace.SMEM)
    sds = jax.ShapeDtypeStruct
    widths = [hi - lo for lo, hi in CUTS]
    new_amps, energies, densities = pl.pallas_call(
        functools.partial(kernel, devices),
        out_shape=[
            sds((PAIR_DEV, npao, npao), BF16),
            sds((PAIR_DEV,), F32),
            sds((OCC_DEV, npao, npao), F32),
        ],
        in_specs=[smem] * 3 + [hbm] * 5,
        out_specs=[hbm, smem, hbm],
        scratch_shapes=[
            pltpu.VMEM((OCC_DEV, npao, naux), BF16),
            pltpu.VMEM((24, naux), jnp.int32),
            pltpu.VMEM((npao, norb), jnp.int32),
            pltpu.VMEM((npao, norb), F32),
            pltpu.VMEM((PAIR_DEV, npao, npao), BF16),
            pltpu.VMEM((norb, 3 * LANE), jnp.int32),
            pltpu.VMEM((norb, 3 * LANE), F32),
            pltpu.VMEM((3, OCC_DEV, npao, 2 * npao), BF16),
            pltpu.VMEM((PAIR_DEV, npao, naux), BF16),
            *[pltpu.VMEM((3, OCC_DEV, npao, w), BF16) for w in widths],
            pltpu.VMEM((PAIR_DEV, npao, npao), F32),
            pltpu.VMEM((PAIR_DEV, npao, npao), F32),
            pltpu.VMEM((PAIR_DEV, npao, npao), F32),
            pltpu.VMEM((npao, NCPL * npao), BF16),
            pltpu.VMEM((npao, NCPL * npao), BF16),
            pltpu.VMEM((OCC_DEV, npao, npao), F32),
            pltpu.VMEM((PAIR_DEV, npao, npao), BF16),
            pltpu.SemaphoreType.DMA((10,)),
            pltpu.SemaphoreType.DMA((4, 2)),
            pltpu.SemaphoreType.DMA((4, 2)),
            pltpu.SemaphoreType.DMA((PAIR_DEV + 1,)),
        ],
        compiler_params=pltpu.CompilerParams(
            collective_id=0, has_side_effects=True, vmem_limit_bytes=60 * 1024 * 1024
        ),
        name="update",
    )(
        pair_partner,
        coupling_list.T,
        coupling_coef.T,
        jnp.swapaxes(blocks, 1, 2),
        aux_domain,
        pao_domain.T,
        pao_gap.T,
        amplitudes,
    )
    return (new_amps, energies, densities)


def solution(mesh):
    return jax.shard_map(
        local,
        mesh=mesh,
        in_specs=(
            P(("orb", "pair"), None, None),
            P(),
            P(),
            P(),
            P(("orb", "pair"), None, None),
            P(),
            P(("orb", "pair"), None),
            P(("orb", "pair"), None),
        ),
        out_specs=(
            P(("orb", "pair"), None, None),
            P(("orb", "pair")),
            P(("orb", "pair"), None, None),
        ),
        check_vma=False,
    )
```

time: 502 us -> 112 us (0.22)
  the two profiles are of different devices: /device:TPU:96 before, /device:TPU:1 now
where the time goes in v2:
time: 112 us
  Pallas kernels  106 us (95%)
  local copies, waits for them, and re-layouts  4.95 us (4%)
    pallas_call x1, Pallas kernels, local(): pl.pallas_call(functools.partial(kernel, devices), out_shape=[sds((PAIR_D...  106 us
    unnamed x7, local copies, waits for them, and re-layouts  4.95 us

profile of v2, /device:TPU:1, one launch (start us, length us, event | category | flops | bytes accessed | tf_op | source)
XLA Modules:
  0.0 112.0 jit_solution(13578660625796140751)
XLA Ops:
  0.6 106.4 %update.1 = (bf16[8,320,320]{2,1,0:T(8,128)(2,1)}, f32[8]{0:T(128)}, f32[4,320,320]{2,1,0:T(8,128)}) custom-call(s32[1024]{0:T(1024)} %partner.1, s32[4,8]{1,0:T(4,128)} %bitcast.8, f32[4,8]{1,0:T(4,128)} %bitcast.9, bf16[4,320,1024]{2,1,0:T(8,128)(2,1)} %bitcast.5, s32[512,1024]{1,0:T(8,128)} %aux_hbm.1, s32[320,512]{1,0:T(8,128)} %bitcast.6, ...), custom_call_target="tpu_custom_call" | custom-call | tf_op jit(solution)/shard_map/update/pallas_call | solution.py:355
  107.1 0.0 copy-start.1
  107.1 0.0 copy-start
  107.1 3.2 %copy.14 = bf16[8,320,320]{2,1,0:T(8,128)(2,1)} copy(bf16[8,320,320]{2,1,0:T(8,128)(2,1)} %get-tuple-element.6) | data formatting | bytes 3276800
  110.3 0.0 copy-done.1
  110.3 0.5 copy.15
  110.8 0.0 copy-done
  110.8 1.3 %copy.16 = f32[4,320,320]{2,1,0:T(8,128)} copy(f32[4,320,320]{2,1,0:T(8,128)S(1)} %copy-done) | data formatting | bytes 3276800
Async XLA Ops:
  107.1 3.2 %copy-start.1 = (f32[8]{0:T(128)S(1)}, f32[8]{0:T(128)}, u32[]{:S(2)}) copy-start(f32[8]{0:T(128)} %get-tuple-element.7) | copy-start | bytes 100
  107.1 3.7 %copy-start = (f32[4,320,320]{2,1,0:T(8,128)S(1)}, f32[4,320,320]{2,1,0:T(8,128)}, u32[]{:S(2)}) copy-start(f32[4,320,320]{2,1,0:T(8,128)} %get-tuple-element.8) | copy-start | bytes 4915204

commit v3 on v2

--- a/solution.py
+++ b/solution.py
@@ -17,7 +17,8 @@
 MESH = pl.DeviceIdType.MESH
 CONTRACT_LAST = (((1,), (1,)), ((), ()))
 CONTRACT_FIRST = (((0,), (0,)), ((), ()))
-CUTS = ((0, 256), (256, 768), (768, 1024))
+AMPS = OCC_DEV
+BACK = OCC_DEV + 1
 
 
 def column(row, rows):
@@ -55,9 +56,9 @@
     pao_hbm,
     gap_hbm,
     amps_hbm,
-    new_hbm,
+    new,
     energy_ref,
-    dens_hbm,
+    acc,
     own,
     aux,
     pao_window,
@@ -67,28 +68,32 @@
     gap,
     amps,
     picked,
-    part0,
-    part1,
-    part2,
-    exch,
+    turned,
+    blocks,
+    result_out,
+    result_in,
     scale_ref,
     base_ref,
     rows_ref,
     cols_ref,
-    acc,
-    new,
     local_sems,
     send_sems,
     recv_sems,
-    out_sems,
 ):
     pairs_axis = lax.axis_size("pair")
     me = lax.axis_index("orb") * pairs_axis + lax.axis_index("pair")
     npao, naux = own.shape[1:]
     norb = aux_hbm.shape[0]
     rest = npao - MAIN
-    parts = (part0, part1, part2)
     has = (me > 0, me < devices - 1)
+    spot = lax.rem(me, 2 * pairs_axis)
+    keeps = (
+        jnp.logical_and(has[0], spot >= pairs_axis),
+        jnp.logical_and(
+            has[1], jnp.logical_or(spot < pairs_axis - 1, spot == 2 * pairs_axis - 1)
+        ),
+    )
+    gives = tuple(jnp.logical_and(h, jnp.logical_not(k)) for h, k in zip(has, keeps))
     peers = tuple(
         (lax.div(at, pairs_axis), lax.rem(at, pairs_axis))
         for at in (lax.rem(me + devices - 1, devices), lax.rem(me + 1, devices))
@@ -105,9 +110,7 @@
                 (amps_hbm, raw),
                 (blocks_hbm, own),
                 (gap_hbm, gap_window),
-                (blocks_hbm.at[:, :, CUTS[0][0] : CUTS[0][1]], part0.at[1]),
-                (blocks_hbm.at[:, :, CUTS[1][0] : CUTS[1][1]], part1.at[1]),
-                (blocks_hbm.at[:, :, CUTS[2][0] : CUTS[2][1]], part2.at[1]),
+                (blocks_hbm, blocks.at[1]),
                 *[
                     (
                         aux_hbm.at[pl.ds(lax.rem(group + groups - 1 + g, groups) * 8, 8)],
@@ -138,12 +141,13 @@
     def _():
         pl.semaphore_wait(barrier, 1)
 
-    def remote(n, side):
-        if n < len(CUTS):
-            src = blocks_hbm.at[:, :, CUTS[n][0] : CUTS[n][1]]
-            dst = parts[n].at[2 - 2 * side]
+    def remote(n, side, back):
+        if not back and isinstance(n, int) and n == AMPS:
+            src, dst = amps.at[1], amps.at[2 - 2 * side]
+        elif back:
+            src, dst = result_out.at[side, n - BACK], result_in.at[1 - side, n - BACK]
         else:
-            src, dst = amps.at[1], amps.at[2 - 2 * side]
+            src, dst = blocks_hbm.at[n], blocks.at[2 - 2 * side, n]
         return pltpu.make_async_remote_copy(
             src_ref=src,
             dst_ref=dst,
@@ -153,28 +157,23 @@
             device_id_type=MESH,
         )
 
-    def start(n):
+    def each(senders, act, back=False):
         for side in range(2):
 
-            @pl.when(has[side])
+            @pl.when(senders[side])
             def _(side=side):
-                remote(n, side).start()
-
-    def sent(n):
-        for side in range(2):
-
-            @pl.when(has[side])
-            def _(side=side):
-                remote(n, side).wait_send()
-
-    def arrived(n):
-        for side in range(2):
-
-            @pl.when(has[1 - side])
-            def _(side=side):
-                remote(n, side).wait_recv()
-
-    start(0)
+                act(side, back)
+
+    def start(n, senders, back=False):
+        each(senders, lambda side, back: remote(n, side, back).start(), back)
+
+    def sent(n, senders, back=False):
+        each(senders, lambda side, back: remote(n, side, back).wait_send(), back)
+
+    def arrived(n, receivers, back=False):
+        each(receivers, lambda side, back: remote(n, 1 - side, back).wait_recv(), back)
+
+    start(0, gives)
 
     def rows_of(window):
         x = window[...]
@@ -208,20 +207,51 @@
 
     loads[2].wait()
     for g in range(3):
-        loads[7 + g].wait()
-
-    def align(p):
-        k = lax.rem(p, OCC_DEV)
-        col = column(aux[pl.ds(me * OCC_DEV + k - aux_start, 1), :], naux)
-        second = wrapped(partner[me * PAIR_DEV + p] - aux_start, aux.shape[0])
-        present = aux[pl.ds(second, 1), :]
+        loads[5 + g].wait()
+
+    def aligned(out, o, other):
+        col = column(aux[pl.ds(me * OCC_DEV + o - aux_start, 1), :], naux)
+        present = aux[pl.ds(other, 1), :]
         for at in range(0, naux, MAIN):
             pick = lanes(col, present[:, at : at + MAIN])
-            picked[p, :, at : at + MAIN] = dot(own[k], pick).astype(BF16)
+            out[:, at : at + MAIN] = dot(own[o], pick).astype(BF16)
+
+    def align(p):
+        second = wrapped(partner[me * PAIR_DEV + p] - aux_start, aux.shape[0])
+        aligned(picked.at[p], lax.rem(p, OCC_DEV), second)
 
     pl.loop(0, 1)(align)
-    start(3)
-    pl.loop(1, PAIR_DEV)(align)
+    start(AMPS, has)
+    for side in range(2):
+
+        @pl.when(keeps[side])
+        def _(side=side):
+            far = me - 1 + 2 * side
+
+            @pl.loop(0, PAIR_DEV)
+            def _(p):
+                o = wrapped(partner[far * PAIR_DEV + p] - me * OCC_DEV, OCC_DEV)
+                first = far * OCC_DEV + lax.rem(p, OCC_DEV) - aux_start
+                aligned(turned.at[side, p], o, first)
+
+    pl.loop(1, PAIR_DEV // 2)(align)
+    busy = jnp.logical_and(*keeps)
+
+    @pl.when(jnp.logical_not(busy))
+    def _():
+        pl.loop(PAIR_DEV // 2, PAIR_DEV)(align)
+
+    def exchange_back(k):
+        for side in range(2):
+
+            @pl.when(keeps[side])
+            def _(side=side):
+                tails = []
+                for n in range(2):
+                    whole = dot(blocks[2 * side, k], turned[side, k + n * OCC_DEV], CONTRACT_LAST)
+                    result_out[side, k, :, n * MAIN : (n + 1) * MAIN] = whole[:, :MAIN].astype(BF16)
+                    tails.append(whole[:, MAIN:])
+                result_out[side, k, :, 2 * MAIN :] = jnp.concatenate(tails, axis=1).astype(BF16)
 
     def amp_of(side, p):
         k, half = lax.rem(p, OCC_DEV), lax.div(p, OCC_DEV)
@@ -246,28 +276,15 @@
         acc[o] = dot(packed, packed, CONTRACT_LAST)
     right_terms(1)
 
-    def block_of(part, p):
-        spot = wrapped(partner[me * PAIR_DEV + p] - (me - 1) * OCC_DEV, 3 * OCC_DEV)
-        return part[lax.div(spot, OCC_DEV), lax.rem(spot, OCC_DEV)]
-
-    def exchange_term(n, p):
-        lo, hi = CUTS[n]
-        return dot(picked[p, :, lo:hi], block_of(parts[n], p), CONTRACT_LAST)
-
-    loads[4].wait()
-    arrived(0)
-
-    @pl.loop(0, PAIR_DEV)
-    def _(p):
-        exch[p] = exchange_term(0, p)
-
-    sent(3)
-    start(1)
-    arrived(3)
+    arrived(0, keeps)
+    exchange_back(0)
+    sent(AMPS, has)
+    start(1, gives)
+    start(2, gives)
+    arrived(AMPS, has)
     low = lax.broadcasted_iota(jnp.int32, (1, 2 * rest), 1) < rest
 
-    @pl.loop(0, PAIR_DEV)
-    def _(p):
+    def couple(p):
         i_row = me * OCC_DEV + lax.rem(p, OCC_DEV)
         j_row = partner[me * PAIR_DEV + p]
         left = column(wanted(tab[pl.ds(i_row, 1), :]), npao)
@@ -309,37 +326,70 @@
             scale_ref[p, :, lo:hi] = jnp.where(keep, half_inverse, F32(0))
             base_ref[p, :, lo:hi] = amp - (denom * amp - coupling[:, lo:hi]) * half_inverse
 
-    start(2)
+    pl.loop(0, 1)(couple)
+    start(BACK, keeps, True)
+    pl.loop(1, 4)(couple)
+    sent(1, gives)
+    start(3, gives)
+    pl.loop(4, 5)(couple)
+    arrived(1, keeps)
+    exchange_back(1)
+    pl.loop(5, 6)(couple)
+    start(BACK + 1, keeps, True)
+    arrived(2, keeps)
+    exchange_back(2)
+    pl.loop(6, 7)(couple)
+    start(BACK + 2, keeps, True)
+    pl.loop(7, 8)(couple)
     right_terms(0)
     right_terms(2)
+    loads[4].wait()
+    arrived(3, keeps)
+    exchange_back(3)
+
+    def finish(k):
+        arrived(BACK + k, gives, True)
+        for n in range(2):
+            p = k + n * OCC_DEV
+            spot = wrapped(partner[me * PAIR_DEV + p] - (me - 1) * OCC_DEV, 3 * OCC_DEV)
+            side, slot = lax.div(spot, OCC_DEV), lax.rem(spot, OCC_DEV)
+            whole = dot(picked[p], blocks[side, slot], CONTRACT_LAST)
+            amp = amps[1, k]
+            tail = amp[:, 2 * MAIN + n * rest : 2 * MAIN + (n + 1) * rest].astype(F32)
+            energy = F32(0)
+            for lo, hi, at, value in (
+                (0, MAIN, n * MAIN, amp[:, n * MAIN : (n + 1) * MAIN].astype(F32)),
+                (MAIN, npao, 2 * MAIN + n * rest, tail),
+            ):
+                exchange = whole[:, lo:hi]
+                for far in range(2):
+                    came = jnp.logical_and(gives[far], side == 2 * far)
+                    other = result_in[far, k, :, at : at + hi - lo].astype(F32)
+                    exchange = jnp.where(came, other, exchange)
+                new[p, :, lo:hi] = (
+                    base_ref[p, :, lo:hi] - scale_ref[p, :, lo:hi] * exchange
+                ).astype(BF16)
+                energy += jnp.sum(exchange * value)
+            energy_ref[p] = energy / npao
+
+    @pl.when(busy)
+    def _():
+        pl.loop(PAIR_DEV // 2, PAIR_DEV // 2 + 1)(align)
+
     acc[...] = acc[...] / npao
-    dens_out = pltpu.make_async_copy(acc, dens_hbm, out_sems.at[PAIR_DEV])
-    dens_out.start()
-
-    loads[5].wait()
-    arrived(1)
-
-    @pl.loop(0, PAIR_DEV)
-    def _(p):
-        exch[p] += exchange_term(1, p)
-
-    loads[6].wait()
-    arrived(2)
-
-    @pl.loop(0, PAIR_DEV)
-    def _(p):
-        whole = exch[p] + exchange_term(2, p)
-        main, tail = amp_of(1, p)
-        new[p] = (base_ref[p] - scale_ref[p] * whole).astype(BF16)
-        energy = jnp.sum(whole[:, :MAIN] * main.astype(F32)) + jnp.sum(whole[:, MAIN:] * tail)
-        energy_ref[p] = energy / npao
-        pltpu.make_async_copy(new.at[p], new_hbm.at[p], out_sems.at[p]).start()
-
-    for p in range(PAIR_DEV):
-        pltpu.make_async_copy(new.at[p], new_hbm.at[p], out_sems.at[p]).wait()
-    dens_out.wait()
-    for n in range(3):
-        sent(n)
+    start(BACK + 3, keeps, True)
+
+    @pl.when(busy)
+    def _():
+        pl.loop(PAIR_DEV // 2 + 1, PAIR_DEV)(align)
+
+    pl.loop(0, 1)(finish)
+    pl.loop(1, OCC_DEV)(finish)
+    sent(0, gives)
+    sent(2, gives)
+    sent(3, gives)
+    for k in range(OCC_DEV):
+        sent(BACK + k, keeps, True)
 
 
 def local(
@@ -350,17 +400,17 @@
     norb = aux_domain.shape[0]
     hbm = pl.BlockSpec(memory_space=pltpu.MemorySpace.HBM)
     smem = pl.BlockSpec(memory_space=pltpu.MemorySpace.SMEM)
+    vmem = pl.BlockSpec(memory_space=pltpu.MemorySpace.VMEM)
     sds = jax.ShapeDtypeStruct
-    widths = [hi - lo for lo, hi in CUTS]
     new_amps, energies, densities = pl.pallas_call(
         functools.partial(kernel, devices),
         out_shape=[
-            sds((PAIR_DEV, npao, npao), BF16),
+            pltpu.VMEM((PAIR_DEV, npao, npao), BF16),
             sds((PAIR_DEV,), F32),
-            sds((OCC_DEV, npao, npao), F32),
+            pltpu.VMEM((OCC_DEV, npao, npao), F32),
         ],
         in_specs=[smem] * 3 + [hbm] * 5,
-        out_specs=[hbm, smem, hbm],
+        out_specs=[vmem, smem, vmem],
         scratch_shapes=[
             pltpu.VMEM((OCC_DEV, npao, naux), BF16),
             pltpu.VMEM((24, naux), jnp.int32),
@@ -371,18 +421,17 @@
             pltpu.VMEM((norb, 3 * LANE), F32),
             pltpu.VMEM((3, OCC_DEV, npao, 2 * npao), BF16),
             pltpu.VMEM((PAIR_DEV, npao, naux), BF16),
-            *[pltpu.VMEM((3, OCC_DEV, npao, w), BF16) for w in widths],
-            pltpu.VMEM((PAIR_DEV, npao, npao), F32),
+            pltpu.VMEM((2, PAIR_DEV, npao, naux), BF16),
+            pltpu.VMEM((3, OCC_DEV, npao, naux), BF16),
+            pltpu.VMEM((2, OCC_DEV, npao, 2 * npao), BF16),
+            pltpu.VMEM((2, OCC_DEV, npao, 2 * npao), BF16),
             pltpu.VMEM((PAIR_DEV, npao, npao), F32),
             pltpu.VMEM((PAIR_DEV, npao, npao), F32),
             pltpu.VMEM((npao, NCPL * npao), BF16),
             pltpu.VMEM((npao, NCPL * npao), BF16),
-            pltpu.VMEM((OCC_DEV, npao, npao), F32),
-            pltpu.VMEM((PAIR_DEV, npao, npao), BF16),
-            pltpu.SemaphoreType.DMA((10,)),
-            pltpu.SemaphoreType.DMA((4, 2)),
-            pltpu.SemaphoreType.DMA((4, 2)),
-            pltpu.SemaphoreType.DMA((PAIR_DEV + 1,)),
+            pltpu.SemaphoreType.DMA((8,)),
+            pltpu.SemaphoreType.DMA((2 * OCC_DEV + 1, 2)),
+            pltpu.SemaphoreType.DMA((2 * OCC_DEV + 1, 2)),
         ],
         compiler_params=pltpu.CompilerParams(
             collective_id=0, has_side_effects=True, vmem_limit_bytes=60 * 1024 * 1024

time: 112 us -> 106 us (0.946)
  the two profiles are of different devices: /device:TPU:1 before, /device:TPU:96 now
where the time goes in v3:
time: 106 us
  Pallas kernels  102 us (96%)
  local copies, waits for them, and re-layouts  3.06 us (3%)
    pallas_call x1, Pallas kernels, local(): pl.pallas_call(functools.partial(kernel, devices), out_shape=[pltpu.VMEM(...  102 us
    unnamed x5, local copies, waits for them, and re-layouts  3.06 us

profile of v3, /device:TPU:96, one launch (start us, length us, event | category | flops | bytes accessed | tf_op | source)
XLA Modules:
  0.0 106.2 jit_solution(13668866859393639666)
XLA Ops:
  0.6 102.5 %update.1 = (bf16[8,320,320]{2,1,0:T(8,128)(2,1)S(1)}, f32[8]{0:T(128)}, f32[4,320,320]{2,1,0:T(8,128)S(1)}) custom-call(s32[1024]{0:T(1024)} %partner.1, s32[4,8]{1,0:T(4,128)} %bitcast.8, f32[4,8]{1,0:T(4,128)} %bitcast.9, bf16[4,320,1024]{2,1,0:T(8,128)(2,1)} %bitcast.5, s32[512,1024]{1,0:T(8,128)} %aux_hbm.1, s32[320,512]{1,0:T(8,128)} %bitcast.6, ...), custom_call_target="tpu_custom_call" | custom-call | tf_op jit(solution)/shard_map/update/pallas_call | solution.py:405
  103.1 1.3 %copy.14 = bf16[8,320,320]{2,1,0:T(8,128)(2,1)} copy(bf16[8,320,320]{2,1,0:T(8,128)(2,1)S(1)} %get-tuple-element.3) | data formatting | bytes 3276800
  104.4 0.0 copy-start
  104.4 1.3 %copy.15 = f32[4,320,320]{2,1,0:T(8,128)} copy(f32[4,320,320]{2,1,0:T(8,128)S(1)} %get-tuple-element.5) | data formatting | bytes 3276800
  105.7 0.0 copy-done
  105.7 0.5 copy.16
Async XLA Ops:
  104.4 1.3 %copy-start = (f32[8]{0:T(128)S(1)}, f32[8]{0:T(128)}, u32[]{:S(2)}) copy-start(f32[8]{0:T(128)} %get-tuple-element.10) | copy-start | bytes 100

commit v4 on v3

--- a/solution.py
+++ b/solution.py
@@ -19,6 +19,9 @@
 CONTRACT_FIRST = (((0,), (0,)), ((), ()))
 AMPS = OCC_DEV
 BACK = OCC_DEV + 1
+LAST = OCC_DEV - 1
+LAST_LOW = BACK + OCC_DEV
+LAST_BACK_LOW = LAST_LOW + 1
 
 
 def column(row, rows):
@@ -142,8 +145,16 @@
         pl.semaphore_wait(barrier, 1)
 
     def remote(n, side, back):
-        if not back and isinstance(n, int) and n == AMPS:
+        number = n if isinstance(n, int) else -1
+        half = npao // 2
+        if number == AMPS:
             src, dst = amps.at[1], amps.at[2 - 2 * side]
+        elif number in (BACK + LAST, LAST_BACK_LOW):
+            rows = slice(0, half) if number == BACK + LAST else slice(half, npao)
+            src, dst = result_out.at[side, LAST, rows], result_in.at[1 - side, LAST, rows]
+        elif number in (LAST, LAST_LOW):
+            rows = slice(0, half) if number == LAST else slice(half, npao)
+            src, dst = blocks_hbm.at[LAST, rows], blocks.at[2 - 2 * side, LAST, rows]
         elif back:
             src, dst = result_out.at[side, n - BACK], result_in.at[1 - side, n - BACK]
         else:
@@ -241,17 +252,20 @@
     def _():
         pl.loop(PAIR_DEV // 2, PAIR_DEV)(align)
 
-    def exchange_back(k):
+    def exchange_back(k, lo=0, hi=npao):
         for side in range(2):
 
             @pl.when(keeps[side])
             def _(side=side):
                 tails = []
                 for n in range(2):
-                    whole = dot(blocks[2 * side, k], turned[side, k + n * OCC_DEV], CONTRACT_LAST)
-                    result_out[side, k, :, n * MAIN : (n + 1) * MAIN] = whole[:, :MAIN].astype(BF16)
+                    whole = dot(
+                        blocks[2 * side, k, lo:hi], turned[side, k + n * OCC_DEV], CONTRACT_LAST
+                    )
+                    at = slice(n * MAIN, (n + 1) * MAIN)
+                    result_out[side, k, lo:hi, at] = whole[:, :MAIN].astype(BF16)
                     tails.append(whole[:, MAIN:])
-                result_out[side, k, :, 2 * MAIN :] = jnp.concatenate(tails, axis=1).astype(BF16)
+                result_out[side, k, lo:hi, 2 * MAIN :] = jnp.concatenate(tails, axis=1).astype(BF16)
 
     def amp_of(side, p):
         k, half = lax.rem(p, OCC_DEV), lax.div(p, OCC_DEV)
@@ -260,8 +274,8 @@
         tail = jnp.where(half == 0, tail, pltpu.roll(tail, rest, 1))
         return main, tail[:, :rest]
 
-    def right_terms(side):
-        @pl.loop(0, PAIR_DEV)
+    def right_terms(side, first=0, last=PAIR_DEV):
+        @pl.loop(first, last)
         def _(p):
             q = lax.rem((me + devices - 1 + side) * PAIR_DEV + p, devices * PAIR_DEV)
             target = partner[q] - me * OCC_DEV
@@ -340,16 +354,20 @@
     exchange_back(2)
     pl.loop(6, 7)(couple)
     start(BACK + 2, keeps, True)
+    sent(2, gives)
+    start(LAST_LOW, gives)
     pl.loop(7, 8)(couple)
     right_terms(0)
-    right_terms(2)
     loads[4].wait()
-    arrived(3, keeps)
-    exchange_back(3)
-
-    def finish(k):
-        arrived(BACK + k, gives, True)
-        for n in range(2):
+    arrived(LAST, keeps)
+    exchange_back(LAST, 0, npao // 2)
+    right_terms(2, 0, 2)
+    start(BACK + LAST, keeps, True)
+    right_terms(2, 2, PAIR_DEV)
+    acc[...] = acc[...] / npao
+
+    def finish(k, parts=(0, 1)):
+        for n in parts:
             p = k + n * OCC_DEV
             spot = wrapped(partner[me * PAIR_DEV + p] - (me - 1) * OCC_DEV, 3 * OCC_DEV)
             side, slot = lax.div(spot, OCC_DEV), lax.rem(spot, OCC_DEV)
@@ -370,26 +388,52 @@
                     base_ref[p, :, lo:hi] - scale_ref[p, :, lo:hi] * exchange
                 ).astype(BF16)
                 energy += jnp.sum(exchange * value)
-            energy_ref[p] = energy / npao
+            energy_ref[pl.ds(p, 1), :] = jnp.full((1, LANE), energy / npao, F32)
+
+    for k in range(LAST):
+        arrived(BACK + k, gives, True)
+
+    arrived(LAST_LOW, keeps)
+    exchange_back(LAST, npao // 2, npao)
+    pl.loop(0, 1)(lambda k: finish(k, (0,)))
+    start(LAST_BACK_LOW, keeps, True)
 
     @pl.when(busy)
     def _():
-        pl.loop(PAIR_DEV // 2, PAIR_DEV // 2 + 1)(align)
-
-    acc[...] = acc[...] / npao
-    start(BACK + 3, keeps, True)
-
-    @pl.when(busy)
-    def _():
-        pl.loop(PAIR_DEV // 2 + 1, PAIR_DEV)(align)
-
-    pl.loop(0, 1)(finish)
-    pl.loop(1, OCC_DEV)(finish)
+        pl.loop(PAIR_DEV // 2, PAIR_DEV)(align)
+
+    pl.loop(0, 1)(lambda k: finish(k, (1,)))
+    pl.loop(1, LAST)(finish)
+    arrived(BACK + LAST, gives, True)
+    arrived(LAST_BACK_LOW, gives, True)
+    pl.loop(LAST, OCC_DEV)(finish)
     sent(0, gives)
-    sent(2, gives)
-    sent(3, gives)
+    sent(LAST, gives)
+    sent(LAST_LOW, gives)
     for k in range(OCC_DEV):
         sent(BACK + k, keeps, True)
+    sent(LAST_BACK_LOW, keeps, True)
+
+
+def write_kernel(new, energy, dens, new_hbm, energy_out, dens_hbm, sems):
+    half = new.shape[1] // 2
+    pieces = [(new, new_hbm, p) for p in range(PAIR_DEV)]
+    pieces += [(dens, dens_hbm, o) for o in range(OCC_DEV)]
+    copies = [
+        pltpu.make_async_copy(
+            src.at[n, part * half : (part + 1) * half],
+            dst.at[n, part * half : (part + 1) * half],
+            sems.at[2 * at + part],
+        )
+        for at, (src, dst, n) in enumerate(pieces)
+        for part in range(2)
+    ]
+    for copy in copies:
+        copy.start()
+    for p in range(PAIR_DEV):
+        energy_out[p] = energy[p, 0]
+    for copy in copies:
+        copy.wait()
 
 
 def local(
@@ -406,11 +450,11 @@
         functools.partial(kernel, devices),
         out_shape=[
             pltpu.VMEM((PAIR_DEV, npao, npao), BF16),
-            sds((PAIR_DEV,), F32),
+            pltpu.VMEM((PAIR_DEV, LANE), F32),
             pltpu.VMEM((OCC_DEV, npao, npao), F32),
         ],
         in_specs=[smem] * 3 + [hbm] * 5,
-        out_specs=[vmem, smem, vmem],
+        out_specs=[vmem, vmem, vmem],
         scratch_shapes=[
             pltpu.VMEM((OCC_DEV, npao, naux), BF16),
             pltpu.VMEM((24, naux), jnp.int32),
@@ -430,8 +474,8 @@
             pltpu.VMEM((npao, NCPL * npao), BF16),
             pltpu.VMEM((npao, NCPL * npao), BF16),
             pltpu.SemaphoreType.DMA((8,)),
-            pltpu.SemaphoreType.DMA((2 * OCC_DEV + 1, 2)),
-            pltpu.SemaphoreType.DMA((2 * OCC_DEV + 1, 2)),
+            pltpu.SemaphoreType.DMA((LAST_BACK_LOW + 1, 2)),
+            pltpu.SemaphoreType.DMA((LAST_BACK_LOW + 1, 2)),
         ],
         compiler_params=pltpu.CompilerParams(
             collective_id=0, has_side_effects=True, vmem_limit_bytes=60 * 1024 * 1024
@@ -447,7 +491,19 @@
         pao_gap.T,
         amplitudes,
     )
-    return (new_amps, energies, densities)
+    return pl.pallas_call(
+        write_kernel,
+        out_shape=[
+            sds((PAIR_DEV, npao, npao), BF16),
+            sds((PAIR_DEV,), F32),
+            sds((OCC_DEV, npao, npao), F32),
+        ],
+        in_specs=[vmem, vmem, vmem],
+        out_specs=[hbm, smem, hbm],
+        scratch_shapes=[pltpu.SemaphoreType.DMA((2 * (PAIR_DEV + OCC_DEV),))],
+        compiler_params=pltpu.CompilerParams(vmem_limit_bytes=1024 * 1024),
+        name="write",
+    )(new_amps, energies, densities)
 
 
 def solution(mesh):

time: 106 us -> 103 us (0.972)
  local copies, waits for them, and re-layouts: 3.06 us -> 0 us
    pallas_call x1, Pallas kernels: 102 us -> 99 us  [local(): pl.pallas_call(functools.partial(kernel, devices), out_shape=[pltpu.VMEM(...]
    unnamed x5 -> x0, local copies, waits for them, and re-layouts: 3.06 us -> none
    pallas_call x0 -> x1, Pallas kernels: none -> 2.63 us  [local(): pl.pallas_call(write_kernel, out_shape=[sds((PAIR_DEV, npao, npao), BF16)...]
where the time goes in v4:
time: 103 us; the launch traced here: 102 us
  Pallas kernels  102 us (99%)
    pallas_call x1, Pallas kernels, local(): pl.pallas_call(functools.partial(kernel, devices), out_shape=[pltpu.VMEM(...  99 us
    pallas_call x1, Pallas kernels, local(): pl.pallas_call(write_kernel, out_shape=[sds((PAIR_DEV, npao, npao), BF16)...  2.63 us

profile of v4, /device:TPU:96, one launch (start us, length us, event | category | flops | bytes accessed | tf_op | source)
XLA Modules:
  0.0 102.5 jit_solution(180528846501586062)
XLA Ops:
  0.6 99.0 %update.1 = (bf16[8,320,320]{2,1,0:T(8,128)(2,1)S(1)}, f32[8,128]{1,0:T(8,128)S(1)}, f32[4,320,320]{2,1,0:T(8,128)S(1)}) custom-call(s32[1024]{0:T(1024)} %partner.1, s32[4,8]{1,0:T(4,128)} %bitcast.8, f32[4,8]{1,0:T(4,128)} %bitcast.9, bf16[4,320,1024]{2,1,0:T(8,128)(2,1)} %bitcast.5, s32[512,1024]{1,0:T(8,128)} %aux_hbm.1, s32[320,512]{1,0:T(8,128)} %bitcast.6, ...), custom_call_target="tpu_custom_call" | custom-call | tf_op jit(solution)/shard_map/update/pallas_call | solution.py:449
  99.7 2.6 %write.1 = (bf16[8,320,320]{2,1,0:T(8,128)(2,1)}, f32[8]{0:T(128)}, f32[4,320,320]{2,1,0:T(8,128)}) custom-call(bf16[8,320,320]{2,1,0:T(8,128)(2,1)S(1)} %get-tuple-element.6.new, f32[8,128]{1,0:T(8,128)S(1)} %get-tuple-element.7.energy, f32[4,320,320]{2,1,0:T(8,128)S(1)} %get-tuple-element.8.dens), custom_call_target="tpu_custom_call" | custom-call | tf_op jit(solution)/shard_map/write/pallas_call | solution.py:494

commit v5 on v4

--- a/solution.py
+++ b/solution.py
@@ -216,6 +216,7 @@
         def _(side=side):
             amps[2 * side] = jnp.zeros_like(amps[2 * side])
 
+    start(AMPS, has)
     loads[2].wait()
     for g in range(3):
         loads[5 + g].wait()
@@ -232,7 +233,6 @@
         aligned(picked.at[p], lax.rem(p, OCC_DEV), second)
 
     pl.loop(0, 1)(align)
-    start(AMPS, has)
     for side in range(2):
 
         @pl.when(keeps[side])
@@ -292,8 +292,8 @@
 
     arrived(0, keeps)
     exchange_back(0)
+    start(1, gives)
     sent(AMPS, has)
-    start(1, gives)
     start(2, gives)
     arrived(AMPS, has)
     low = lax.broadcasted_iota(jnp.int32, (1, 2 * rest), 1) < rest

time: 103 us -> 101 us (0.981)
  Pallas kernels: 102 us -> 99.8 us
    pallas_call x1, Pallas kernels: 99 us -> 97.1 us  [local(): pl.pallas_call(functools.partial(kernel, devices), out_shape=[pltpu.VMEM(...]
where the time goes in v5:
time: 101 us
  Pallas kernels  99.8 us (99%)
    pallas_call x1, Pallas kernels, local(): pl.pallas_call(functools.partial(kernel, devices), out_shape=[pltpu.VMEM(...  97.1 us
    pallas_call x1, Pallas kernels, local(): pl.pallas_call(write_kernel, out_shape=[sds((PAIR_DEV, npao, npao), BF16)...  2.63 us

profile of v5, /device:TPU:96, one launch (start us, length us, event | category | flops | bytes accessed | tf_op | source)
XLA Modules:
  0.0 100.6 jit_solution(9724974203176677682)
XLA Ops:
  0.6 97.1 %update.1 = (bf16[8,320,320]{2,1,0:T(8,128)(2,1)S(1)}, f32[8,128]{1,0:T(8,128)S(1)}, f32[4,320,320]{2,1,0:T(8,128)S(1)}) custom-call(s32[1024]{0:T(1024)} %partner.1, s32[4,8]{1,0:T(4,128)} %bitcast.8, f32[4,8]{1,0:T(4,128)} %bitcast.9, bf16[4,320,1024]{2,1,0:T(8,128)(2,1)} %bitcast.5, s32[512,1024]{1,0:T(8,128)} %aux_hbm.1, s32[320,512]{1,0:T(8,128)} %bitcast.6, ...), custom_call_target="tpu_custom_call" | custom-call | tf_op jit(solution)/shard_map/update/pallas_call | solution.py:449
  97.8 2.6 %write.1 = (bf16[8,320,320]{2,1,0:T(8,128)(2,1)}, f32[8]{0:T(128)}, f32[4,320,320]{2,1,0:T(8,128)}) custom-call(bf16[8,320,320]{2,1,0:T(8,128)(2,1)S(1)} %get-tuple-element.6.new, f32[8,128]{1,0:T(8,128)S(1)} %get-tuple-element.7.energy, f32[4,320,320]{2,1,0:T(8,128)S(1)} %get-tuple-element.8.dens), custom_call_target="tpu_custom_call" | custom-call | tf_op jit(solution)/shard_map/write/pallas_call | solution.py:494
